TPU v7x, 256 devices: a whole 4x4x8 slice. The times are simulated.
256 devices in a mesh: aux: 32 (over y, x, core), orb: 8 (over z).
Axes of the slice: x: 4, y: 4, z: 8, core: 2. Of those that a mesh axis runs over, the one named last changes fastest.
Arguments:
- band_pattern: int32 [256, 8], P('aux'), may hold values 0 or 1
- density_in: bfloat16 [256, 8, 128, 128], P('aux', 'orb')
- field_terms: bfloat16 [2, 256, 8, 128, 128], P(None, 'aux', 'orb'), may hold values from -3 to 3
- fit_blocks: int32 [1], replicated, may hold values from 0 to 255
- tensor: bfloat16 [1, 3072, 8, 16384], P(None, 'aux', 'orb'), may hold values from -0.015625 to 0.015625
- metric_inv: float32 [1, 3072, 3072], P(None, 'aux')
Outputs:
- response: bfloat16 [2, 256, 8, 128, 128], P(None, 'aux', 'orb')
- coefficients: float32 [1, 2, 3072], P(None, None, 'aux')
All inputs are finite; a program needn't handle non-finite values. No bound on the sum of `band_pattern` on one device may be relied on, other than what follows from the above.
Results may differ from a plain program's by a relative error of at most 0.0055.
Values may be sent and summed in bfloat16 or wider, within the bound.
A program may use at most 192 MiB of HBM per device.

v0:
```python
import jax
import jax.numpy as jnp
from jax import lax
from jax.sharding import PartitionSpec as P


def padded_2(block, sides, width):
    for axis, dim in sides:
        count = lax.axis_size(axis)
        forward = [(i, i + 1) for i in range(count - 1)]
        backward = [(target, source) for source, target in forward]
        low = lax.ppermute(
            lax.slice_in_dim(block, block.shape[dim] - width, None, axis=dim), axis, forward
        )
        high = lax.ppermute(lax.slice_in_dim(block, 0, width, axis=dim), axis, backward)
        block = jnp.concatenate([low, block, high], axis=dim)
    return block


def sent_to_all(x, axis):
    copies = jnp.broadcast_to(x, (lax.axis_size(axis), *x.shape))
    return lax.all_to_all(copies, axis, split_axis=0, concat_axis=0, tiled=True)


def over_copies(x, axis):
    everything = sent_to_all(x, axis)
    return jnp.sum(everything.astype(jnp.float32), axis=0)


def over_copies_2(x, axis):
    everything = sent_to_all(x, axis)
    return jnp.sum(everything, axis=0)


def joined_along(pieces, dim):
    pieces = jnp.moveaxis(pieces, 0, dim)
    lengths = pieces.shape
    return pieces.reshape(*lengths[:dim], lengths[dim] * lengths[dim + 1], *lengths[dim + 2 :])


def gathered_copies(x, axis, dim):
    pieces = sent_to_all(x, axis)
    return joined_along(pieces, dim)


def slide_slots(blocks, offset):
    slot_count = blocks.shape[2]
    if offset >= 0:
        padded = jnp.pad(blocks, ((0, 0), (0, 0), (offset, 0), (0, 0), (0, 0)))
        return padded[:, :, :slot_count]
    padded = jnp.pad(blocks, ((0, 0), (0, 0), (0, -offset), (0, 0), (0, 0)))
    return padded[:, :, -offset : -offset + slot_count]


def band_keep(band_pattern, first_row, total_rows):
    slot_count = band_pattern.shape[1]
    half_band = slot_count // 2
    row_ids = first_row + jnp.arange(band_pattern.shape[0], dtype=jnp.int32)[:, None]
    columns = row_ids + jnp.arange(slot_count, dtype=jnp.int32)[None, :] - half_band
    return (band_pattern == 1) & (columns >= 0) & (columns < total_rows)


def own_slot_product(factor_left, right_rims, my_slot):
    count_rows = factor_left.shape[1]
    slot_count = factor_left.shape[2]
    half_band = slot_count // 2
    lead_count = right_rims.shape[0]
    total = None
    for stride in range(slot_count):
        source_slot = my_slot - stride + half_band
        inside = (source_slot >= 0) & (source_slot < slot_count)
        starts = (
            jnp.int32(0),
            jnp.int32(stride),
            jnp.clip(source_slot, 0, slot_count - 1),
            jnp.int32(0),
            jnp.int32(0),
        )
        sizes = (lead_count, count_rows, 1, right_rims.shape[3], right_rims.shape[4])
        picked = lax.dynamic_slice(right_rims, starts, sizes)[:, :, 0]
        picked = jnp.where(inside, picked, jnp.zeros((), picked.dtype))
        product = jnp.matmul(factor_left[:, :, stride], picked, preferred_element_type=jnp.float32)
        total = product if total is None else total + product
    return total


def all_slot_product(factor_left, right_rims):
    count_rows = factor_left.shape[1]
    slot_count = factor_left.shape[2]
    half_band = slot_count // 2
    total = None
    for stride in range(slot_count):
        source = slide_slots(right_rims[:, stride : stride + count_rows], stride - half_band)
        product = jnp.matmul(
            factor_left[:, :, stride : stride + 1], source, preferred_element_type=jnp.float32
        )
        total = product if total is None else total + product
    return total


def rim_fields(field_rows, half_band):
    return padded_2(field_rows, (("aux", 1),), half_band)


def on_device(band_pattern, density_in, field_terms, fit_blocks, tensor, metric_inv):
    count_rows = density_in.shape[0]
    slot_count = lax.axis_size("orb")
    half_band = slot_count // 2
    total_rows = count_rows * lax.axis_size("aux")
    first_row = lax.axis_index("aux") * count_rows
    my_slot = lax.axis_index("orb")
    keep_all = band_keep(band_pattern, first_row, total_rows)
    keep_own = lax.dynamic_index_in_dim(keep_all, my_slot, 1, keepdims=True)[None, :, :, None, None]
    keep_out = keep_own[:, :, 0]
    zero_half = jnp.zeros((), jnp.bfloat16)
    density = jnp.where(keep_own, density_in[None], zero_half)
    perturbed = jnp.where(keep_own, field_terms, zero_half)
    stacked = jnp.concatenate([density, perturbed], 0)
    whole_rows = lax.all_gather(stacked, "orb", axis=2, tiled=True)
    deep_rows = padded_2(whole_rows[0:1], (("aux", 1),), 2 * half_band)
    field_rows = rim_fields(whole_rows[1:], half_band)
    pattern_wide = padded_2(band_pattern, (("aux", 0),), half_band)
    keep_wide = band_keep(pattern_wide, first_row - half_band, total_rows)[None, :, :, None, None]
    density_rims = deep_rows[:, half_band : half_band + count_rows + 2 * half_band]
    cross_term = own_slot_product(whole_rows[0:1], field_rows, my_slot)
    right_term = own_slot_product(whole_rows[1:], density_rims, my_slot)
    first_order = jnp.where(keep_out, cross_term + right_term, 0.0).astype(jnp.bfloat16)
    square_wide = all_slot_product(density_rims, deep_rows)
    square_rims = jnp.where(keep_wide, square_wide, 0.0).astype(jnp.bfloat16)
    square_rows = square_rims[:, half_band : half_band + count_rows]
    order_rows = lax.all_gather(first_order[:, :, None], "orb", axis=2, tiled=True)
    order_rims = rim_fields(order_rows, half_band)
    second = own_slot_product(square_rows, order_rims, my_slot) + own_slot_product(
        order_rows, square_rims, my_slot
    )
    response = jnp.where(keep_out, 2.0 * first_order.astype(jnp.float32) - second, 0.0).astype(
        jnp.bfloat16
    )[:, :, None]
    owner_row = fit_blocks // count_rows
    local_row = fit_blocks % count_rows
    own_piece = jnp.take(response, local_row, axis=1)
    owner_flag = (owner_row == lax.axis_index("aux"))[None, :, None, None, None]
    contrib = jnp.where(owner_flag, own_piece, zero_half).astype(jnp.float32)
    fitted = (
        over_copies(contrib.astype(jnp.bfloat16), "aux").astype(jnp.float32).astype(jnp.bfloat16)
    )
    flat_blocks = fitted.reshape(fitted.shape[0], fitted.shape[1], -1)
    integrals = tensor.reshape(tensor.shape[0], tensor.shape[1], -1)
    partial_value = jnp.einsum(
        "kfm,fpm->fkp", flat_blocks, integrals, preferred_element_type=jnp.float32
    )
    summed = over_copies_2(partial_value, "orb")
    full_sums = gathered_copies(summed, "aux", 2)
    coefficients = jnp.einsum(
        "fpq,fkq->fkp", metric_inv, full_sums, precision=lax.Precision.HIGHEST
    )
    return (response, coefficients)


def solution(mesh):
    in_specs = (
        P("aux", None),
        P("aux", "orb", None, None),
        P(None, "aux", "orb", None, None),
        P(),
        P(None, "aux", "orb", None),
        P(None, "aux", None),
    )
    out_specs = (P(None, "aux", "orb", None, None), P(None, None, "aux"))
    return jax.shard_map(
        on_device, mesh=mesh, in_specs=in_specs, out_specs=out_specs, check_vma=False
    )
```

profile of v0, /device:TPU:1, one launch (start us, length us, event | category | flops | bytes accessed | tf_op | source)
XLA Modules:
  0.0 341.7 jit_solution(3902713181150019706)
XLA Ops:
  7.2 0.9 fusion.251
  8.3 1.1 copy_select_fusion
  9.5 1.0 bitcast_select_fusion
  10.6 0.9 copy.129
  11.6 78.4 %all-gather.4.cloned.1.call-done = bf16[3,8,8,128,128]{4,3,1,0,2:T(8,128)(2,1)} async-done(((bf16[3,8,1,128,128]{4,3,1,0,2:T(8,128)(2,1)}), bf16[3,8,8,128,128]{4,3,1,0,2:T(8,128)(2,1)}) %all-gather.4.cloned.1.call-update) | async-done | bytes 6291472 | tf_op jit(solution)/shard_map/all_gather | solution.py:119
  90.0 3.2 slice_bitcast_fusion
  93.2 3.6 %collective-permute-start.2 = (bf16[1,8,8,128,128]{4,3,0,1,2:T(8,128)(2,1)}, bf16[1,8,8,128,128]{4,3,0,1,2:T(8,128)(2,1)}, u32[]{:S(2)}, u32[]{:S(2)}) collective-permute-start(bf16[1,8,8,128,128]{4,3,0,1,2:T(8,128)(2,1)} %slice_bitcast_fusion), channel_id=1, source_target_pairs={{0,8},{8,16},{16,24},{24,32},{32,40},{40,48},{48,56},{56,64},{64,7... | collective-permute-start | bytes 6291464 | tf_op jit(solution)/shard_map/ppermute | solution.py:12
  96.9 2.0 collective-permute-start.3
  98.9 2.9 fusion.315
  101.8 1.6 copy.226
  103.4 3.6 %collective-permute-start = (bf16[2,4,8,128,128]{4,3,0,1,2:T(8,128)(2,1)}, bf16[2,4,8,128,128]{4,3,0,1,2:T(8,128)(2,1)}, u32[]{:S(2)}, u32[]{:S(2)}) collective-permute-start(bf16[2,4,8,128,128]{4,3,0,1,2:T(8,128)(2,1)} %copy.226), channel_id=1, source_target_pairs={{0,8},{8,16},{16,24},{24,32},{32,40},{40,48},{48,56},{56,64},{64,7... | collective-permute-start | bytes 6291464 | tf_op jit(solution)/shard_map/ppermute | solution.py:12
  107.1 2.1 collective-permute-start.1
  109.3 1.9 fusion.314
  111.2 8.9 %collective-permute-done.2 = bf16[1,8,8,128,128]{4,3,0,1,2:T(8,128)(2,1)} collective-permute-done((bf16[1,8,8,128,128]{4,3,0,1,2:T(8,128)(2,1)}, bf16[1,8,8,128,128]{4,3,0,1,2:T(8,128)(2,1)}, u32[]{:S(2)}, u32[]{:S(2)}) %collective-permute-start.2) | collective-permute-done | bytes 2097184 | tf_op jit(solution)/shard_map/ppermute | solution.py:12
  120.1 4.4 %collective-permute-done.3 = bf16[1,8,8,128,128]{4,3,0,1,2:T(8,128)(2,1)} collective-permute-done((bf16[1,8,8,128,128]{4,3,0,1,2:T(8,128)(2,1)}, bf16[1,8,8,128,128]{4,3,0,1,2:T(8,128)(2,1)}, u32[]{:S(2)}, u32[]{:S(2)}) %collective-permute-start.3) | collective-permute-done | bytes 2097184 | tf_op jit(solution)/shard_map/ppermute | solution.py:15
  124.5 3.7 %pad_maximum_fusion = bf16[1,24,8,128,128]{4,3,0,1,2:T(8,128)(2,1)S(1)} fusion(bf16[1,8,8,128,128]{4,3,0,1,2:T(8,128)(2,1)} %collective-permute-done.3, bf16[1,8,8,128,128]{4,3,0,1,2:T(8,128)(2,1)} %slice_bitcast_fusion, bf16[1,8,8,128,128]{4,3,0,1,2:T(8,128)(2,1)} %collective-permute-done.2), kind=kLoop, calls=%fused_computation.4 | loop fusion | flops 6291456 | bytes 12582912 | tf_op jit(solution)/shard_map/concatenate | solution.py:16
  128.2 11.0 %fusion.313 = (bf16[1,16,8,128,128]{4,3,0,1,2:T(8,128)(2,1)}, bf16[16,8,128,128]{3,2,0,1:T(8,128)(2,1)}, bf16[1,16,8,128,128]{4,3,0,1,2:T(8,128)(2,1)}, bf16[1,1...) fusion(bf16[1,24,8,128,128]{4,3,0,1,2:T(8,128)(2,1)S(1)} %pad_m, ...), kind=kLoop, calls=%fused_computation.404 | loop fusion | bytes 62914560 | tf_op jit(solution)/shard_map/slice | solution.py:93
  139.2 0.5 copy-done.1
  139.9 1.3 convolution_add_fusion.20
  141.3 1.3 collective-permute-done
  142.6 1.7 constant_dynamic-update-slice_fusion.1
  146.0 0.6 copy_dynamic-update-slice_fusion
  146.6 0.4 collective-permute-done.1
  147.0 2.0 constant_dynamic-update-slice_fusion
  151.5 1.1 fusion.40
  152.7 4.0 %collective-permute-start.4 = (s32[4,8]{1,0:T(4,128)S(1)}, s32[4,8]{1,0:T(4,128)S(1)}, u32[]{:S(2)}, u32[]{:S(2)}) collective-permute-start(s32[4,8]{1,0:T(4,128)S(1)} %get-tuple-element.43), channel_id=1, source_target_pairs={{0,8},{8,16},{16,24},{24,32},{32,40},{40,48},{48,56},{56,64},{64,7... | collective-permute-start | bytes 392 | tf_op jit(solution)/shard_map/ppermute | solution.py:12
  156.7 2.1 collective-permute-start.5
  159.5 2.1 collective-permute-done.5
  161.7 3.7 %fusion.4 = (bf16[16,8,128,128]{3,2,0,1:T(8,128)(2,1)S(1)}, bf16[16,8,128,128]{3,2,0,1:T(8,128)(2,1)S(1)}) fusion(bf16[1,16,8,128,128]{4,3,0,1,2:T(8,128)(2,1)} %get-tuple-element.28, bf16[1,16,8,128,128]{4,3,0,1,2:T(8,128)(2,1)} %get-tuple-element.25), kind=kLoop, calls=%fused_computation.13 | loop fusion | bytes 16777216 | tf_op jit(solution)/shard_map/squeeze | solution.py:94
  165.4 0.5 copy-done.7
  165.9 3.4 fusion.2
  169.3 1.0 slice-done.1
  170.3 4.3 %fusion.22 = f32[16,128,8,128]{3,1,2,0:T(8,128)} fusion(bf16[1,24,8,128,128]{4,3,0,1,2:T(8,128)(2,1)S(1)} %bitcast.473, bf16[1,16,8,128,128]{4,3,0,1,2:T(8,128)(2,1)S(1)} %copy-done.6), kind=kOutput, calls=%fused_computation.32 | convolution fusion | flops 536870912 | bytes 13107200 | tf_op jit(solution)/shard_map/dot_general | solution.py:94
  174.6 4.5 %fusion.12 = f32[16,128,8,128]{3,1,2,0:T(8,128)} fusion(bf16[16,8,128,128]{3,2,0,1:T(8,128)(2,1)S(1)} %get-tuple-element.48, bf16[1,24,8,128,128]{4,3,0,1,2:T(8,128)(2,1)S(1)} %bitcast.473), kind=kOutput, calls=%fused_computation.22 | convolution fusion | flops 536870912 | bytes 13107200 | tf_op jit(solution)/shard_map/dot_general | solution.py:94
  179.2 4.5 %fusion.14 = f32[16,128,8,128]{3,1,2,0:T(8,128)} fusion(bf16[16,8,128,128]{3,2,0,1:T(8,128)(2,1)S(1)} %get-tuple-element.46, bf16[1,24,8,128,128]{4,3,0,1,2:T(8,128)(2,1)S(1)} %bitcast.473), kind=kOutput, calls=%fused_computation.24 | convolution fusion | flops 536870912 | bytes 13107200 | tf_op jit(solution)/shard_map/dot_general | solution.py:94
  183.6 4.5 %fusion.18 = f32[16,128,8,128]{3,1,2,0:T(8,128)} fusion(bf16[16,8,128,128]{3,2,0,1:T(8,128)(2,1)S(1)} %get-tuple-element.45, bf16[1,24,8,128,128]{4,3,0,1,2:T(8,128)(2,1)S(1)} %bitcast.473), kind=kOutput, calls=%fused_computation.28 | convolution fusion | flops 536870912 | bytes 13107200 | tf_op jit(solution)/shard_map/dot_general | solution.py:94
  188.2 4.5 %fusion.20 = f32[16,128,8,128]{3,1,2,0:T(8,128)} fusion(bf16[16,8,128,128]{3,2,0,1:T(8,128)(2,1)S(1)} %get-tuple-element.47, bf16[1,24,8,128,128]{4,3,0,1,2:T(8,128)(2,1)S(1)} %bitcast.473), kind=kOutput, calls=%fused_computation.30 | convolution fusion | flops 536870912 | bytes 13107200 | tf_op jit(solution)/shard_map/dot_general | solution.py:94
  192.7 4.5 %fusion.16 = f32[16,128,8,128]{3,1,2,0:T(8,128)} fusion(bf16[16,8,128,128]{3,2,0,1:T(8,128)(2,1)S(1)} %copy-done.5, bf16[1,24,8,128,128]{4,3,0,1,2:T(8,128)(2,1)S(1)} %bitcast.473), kind=kOutput, calls=%fused_computation.26 | convolution fusion | flops 536870912 | bytes 13107200 | tf_op jit(solution)/shard_map/dot_general | solution.py:94
  197.2 5.9 %fusion.24 = f32[16,128,8,128]{3,1,2,0:T(8,128)} fusion(bf16[1,24,8,128,128]{4,3,0,1,2:T(8,128)(2,1)S(1)} %bitcast.473, bf16[1,8,8,128,128]{4,3,0,1,2:T(8,128)(2,1)} %slice_bitcast_fusion, bf16[1,8,8,128,128]{4,3,0,1,2:T(8,128)(2,1)} %collective-permute-done.2), kind=kOutput, calls=%fused_computation.34 | convolution fusion | flops 553648128 | bytes 13107200 | tf_op jit(solution)/shard_map/dot_general | solution.py:94
  203.1 4.2 %all-gather.6.cloned.1.call-done = bf16[2,8,1024,128]{3,2,0,1:T(8,128)(2,1)} async-done(((bf16[2,8,128,128]{3,2,0,1:T(8,128)(2,1)}), bf16[2,8,1024,128]{3,2,0,1:T(8,128)(2,1)}) %all-gather.6.cloned.1.call-update) | async-done | bytes 4194320 | tf_op jit(solution)/shard_map/all_gather | solution.py:131
  207.2 5.1 %fusion.316 = (bf16[2,4,8,128,128]{4,3,0,1,2:T(8,128)(2,1)}, bf16[2,4,8,128,128]{4,3,0,1,2:T(8,128)(2,1)}) fusion(bf16[2,8,8,128,128]{4,3,2,0,1:T(8,128)(2,1)} %bitcast.476), kind=kLoop, calls=%fused_computation.407 | loop fusion | bytes 8388608 | tf_op jit(solution)/shard_map/slice | solution.py:15
  212.3 3.8 %collective-permute-start.6 = (bf16[2,4,8,128,128]{4,3,0,1,2:T(8,128)(2,1)}, bf16[2,4,8,128,128]{4,3,0,1,2:T(8,128)(2,1)S(1)}, u32[]{:S(2)}, u32[]{:S(2)}) collective-permute-start(bf16[2,4,8,128,128]{4,3,0,1,2:T(8,128)(2,1)} %get-tuple-element.42), channel_id=1, source_target_pairs={{0,8},{8,16},{16,24},{24,32},{32,40},{40,48},{48,56},{56,64},{64,7... | collective-permute-start | bytes 6291464 | tf_op jit(solution)/shard_map/ppermute | solution.py:12
  216.1 20.1 %select_convert_fusion = bf16[16,128,8,128]{3,1,2,0:T(8,128)(2,1)} fusion(f32[16,128,8,128]{3,1,2,0:T(8,128)} %fusion.12, f32[16,128,8,128]{3,1,2,0:T(8,128)} %fusion.14, f32[16,128,8,128]{3,1,2,0:T(8,128)} %fusion.16, f32[16,128,8,128]{3,1,2,0:T(8,128)} %fusion.18, f32[16,128,8,128]{3,1,2,0:T(8,128)S(1)} %copy-done.3, f32[16,128,8,128]{3,1,2,0:T(8,128)} %fusion.24, ...), kind=kOutput, calls=%fused_computation.3 | convolution fusion | flops 555745280 | bytes 67633280 | tf_op jit(solution)/shard_map/dot_general | solution.py:94
  236.2 2.4 collective-permute-start.7
  238.6 1.2 fusion.46
  239.9 1.2 convolution_add_fusion.6
  241.1 0.3 convolution_add_fusion.5
  241.4 0.3 convolution_add_fusion.4
  241.7 0.3 convolution_add_fusion.3
  242.0 0.3 convolution_add_fusion.2
  242.9 0.6 constant_dynamic-update-slice_fusion.3
  243.5 20.5 %collective-permute-done.7 = bf16[2,4,8,128,128]{4,3,0,1,2:T(8,128)(2,1)S(1)} collective-permute-done((bf16[2,4,8,128,128]{4,3,0,1,2:T(8,128)(2,1)}, bf16[2,4,8,128,128]{4,3,0,1,2:T(8,128)(2,1)S(1)}, u32[]{:S(2)}, u32[]{:S(2)}) %collective-permute-start.7) | collective-permute-done | bytes 2097184 | tf_op jit(solution)/shard_map/ppermute | solution.py:15
  266.8 0.4 fusion.39
  267.3 0.8 copy-done.9
  268.1 0.5 broadcast_in_dim.168
  268.6 36.8 %all_to_all.15 = bf16[32,2,1,1,128,128]{5,4,3,2,1,0:T(8,128)(2,1)} all-to-all(bf16[32,2,1,1,128,128]{5,4,3,2,1,0:T(8,128)(2,1)S(1)} %broadcast_in_dim.168), channel_id=1, replica_groups=mesh['aux'=32,'orb'=8] {'aux'}, dimensions={0} | all-to-all | bytes 4194304 | tf_op jit(solution)/shard_map/all_to_all | solution.py:22
  305.4 1.9 reduce_sum.21
  307.3 0.9 fusion.28
  308.2 10.4 %all_to_all.16 = f32[8,1,2,96]{3,2,1,0:T(2,128)S(1)} all-to-all(f32[8,1,2,96]{3,2,1,0:T(2,128)S(1)} %broadcast_in_dim.169), channel_id=1, replica_groups=mesh['aux'=32,'orb'=8] {'orb'}, dimensions={0} | all-to-all | bytes 12288 | tf_op jit(solution)/shard_map/all_to_all | solution.py:22
  318.7 0.6 broadcast_in_dim.170
  319.3 5.3 %all-to-all-start.2 = ((f32[32,1,2,96]{3,2,1,0:T(2,128)}), f32[32,1,2,96]{3,2,1,0:T(2,128)S(1)}, u32[]{:S(2)}, u32[]{:S(2)}) async-start(f32[32,1,2,96]{3,2,1,0:T(2,128)} %broadcast_in_dim.170), calls=%async_computation.2 | async-start | bytes 65536 | tf_op jit(solution)/shard_map/all_to_all | solution.py:22
  324.6 1.9 copy.172
  326.5 5.5 %all-to-all-done.2 = f32[32,1,2,96]{3,2,1,0:T(2,128)S(1)} async-done(((f32[32,1,2,96]{3,2,1,0:T(2,128)}), f32[32,1,2,96]{3,2,1,0:T(2,128)S(1)}, u32[]{:S(2)}, u32[]{:S(2)}) %all-to-all-start.2) | async-done | bytes 24608 | tf_op jit(solution)/shard_map/all_to_all | solution.py:22
  332.0 2.9 fusion.43
  (83 shorter events, 8.5 us)
Async XLA Ops:
  7.2 300.2 %copy-start = (bf16[1,96,1,16384]{3,1,2,0:T(8,128)(2,1)S(1)}, bf16[1,96,1,16384]{3,1,2,0:T(8,128)(2,1)}, u32[]{:S(2)}) copy-start(bf16[1,96,1,16384]{3,1,2,0:T(8,128)(2,1)} %param.10) | copy-start | bytes 9437188
  7.2 82.8 %all-gather.4.cloned.1.call-start = ((), (), s32[]{:S(2)}) async-start(), calls=%async_computation.3 | async-start | bytes 7077888 | tf_op jit(solution)/shard_map/all_gather | solution.py:119
  11.6 195.7 %all-gather.6.cloned.1.call-start = ((), (), s32[]{:S(2)}) async-start(), calls=%async_computation.4 | async-start | bytes 4718592 | tf_op jit(solution)/shard_map/all_gather | solution.py:131
  93.2 26.9 %collective-permute-start.2 = (bf16[1,8,8,128,128]{4,3,0,1,2:T(8,128)(2,1)}, bf16[1,8,8,128,128]{4,3,0,1,2:T(8,128)(2,1)}, u32[]{:S(2)}, u32[]{:S(2)}) collective-permute-start(bf16[1,8,8,128,128]{4,3,0,1,2:T(8,128)(2,1)} %slice_bitcast_fusion), channel_id=1, source_target_pairs={{0,8},{8,16},{16,24},{24,32},{32,40},{40,48},{48,56},{56,64},{64,7... | collective-permute-start | bytes 6291464 | tf_op jit(solution)/shard_map/ppermute | solution.py:12
  96.9 27.7 %collective-permute-start.3 = (bf16[1,8,8,128,128]{4,3,0,1,2:T(8,128)(2,1)}, bf16[1,8,8,128,128]{4,3,0,1,2:T(8,128)(2,1)}, u32[]{:S(2)}, u32[]{:S(2)}) collective-permute-start(bf16[1,8,8,128,128]{4,3,0,1,2:T(8,128)(2,1)} %slice_bitcast_fusion), channel_id=1, source_target_pairs={{8,0},{16,8},{24,16},{32,24},{40,32},{48,40},{56,48},{64,56},{72,6... | collective-permute-start | bytes 6291464 | tf_op jit(solution)/shard_map/ppermute | solution.py:15
  98.9 10.4 %slice-start.2 = ((s8[6291456]{0:T(1024)(128)(4,1)}), s8[4194304]{0:T(1024)(128)(4,1)S(1)}, s32[]{:S(2)}) async-start(s8[6291456]{0:T(1024)(128)(4,1)} %bitcast.474), calls=%async_computation.7 | async-start | bytes 8388608
  101.8 7.5 %slice-start.3 = ((s8[6291456]{0:T(1024)(128)(4,1)}), s8[2097152]{0:T(1024)(128)(4,1)S(1)}, s32[]{:S(2)}) async-start(s8[6291456]{0:T(1024)(128)(4,1)} %bitcast.474), calls=%async_computation.8 | async-start | bytes 4194304
  103.4 39.2 %collective-permute-start = (bf16[2,4,8,128,128]{4,3,0,1,2:T(8,128)(2,1)}, bf16[2,4,8,128,128]{4,3,0,1,2:T(8,128)(2,1)}, u32[]{:S(2)}, u32[]{:S(2)}) collective-permute-start(bf16[2,4,8,128,128]{4,3,0,1,2:T(8,128)(2,1)} %copy.226), channel_id=1, source_target_pairs={{0,8},{8,16},{16,24},{24,32},{32,40},{40,48},{48,56},{56,64},{64,7... | collective-permute-start | bytes 6291464 | tf_op jit(solution)/shard_map/ppermute | solution.py:12
  107.1 39.9 %collective-permute-start.1 = (bf16[2,4,8,128,128]{4,3,0,1,2:T(8,128)(2,1)S(1)}, bf16[2,4,8,128,128]{4,3,0,1,2:T(8,128)(2,1)}, u32[]{:S(2)}, u32[]{:S(2)}) collective-permute-start(bf16[2,4,8,128,128]{4,3,0,1,2:T(8,128)(2,1)S(1)} %copy.228), channel_id=1, source_target_pairs={{8,0},{16,8},{24,16},{32,24},{40,32},{48,40},{56,48},{64,56},{72,6... | collective-permute-start | bytes 6291464 | tf_op jit(solution)/shard_map/ppermute | solution.py:15
  128.2 11.5 %copy-start.1 = (bf16[1,24,8,128,128]{4,3,0,1,2:T(8,128)(2,1)}, bf16[1,24,8,128,128]{4,3,0,1,2:T(8,128)(2,1)S(1)}, u32[]{:S(2)}) copy-start(bf16[1,24,8,128,128]{4,3,0,1,2:T(8,128)(2,1)S(1)} %pad_maximum_fusion) | copy-start | bytes 18874372
  139.6 4.7 %copy-start.15 = (bf16[2,8,1,128,128]{4,3,1,0,2:T(8,128)(2,1)S(1)}, bf16[2,8,1,128,128]{4,3,1,0,2:T(8,128)(2,1)}, u32[]{:S(2)}) copy-start(bf16[2,8,1,128,128]{4,3,1,0,2:T(8,128)(2,1)} %get-tuple-element.35) | copy-start | bytes 1572868
  141.3 3.4 copy-start.14
  141.3 3.7 %copy-start.13 = (bf16[2,8,1,128,128]{4,3,1,0,2:T(8,128)(2,1)S(1)}, bf16[2,8,1,128,128]{4,3,1,0,2:T(8,128)(2,1)}, u32[]{:S(2)}) copy-start(bf16[2,8,1,128,128]{4,3,1,0,2:T(8,128)(2,1)} %get-tuple-element.33) | copy-start | bytes 1572868
  144.3 1.0 copy-start.12
  144.7 1.1 copy-start.11
  150.5 1.0 copy-start.10
  150.8 1.9 copy-start.16
  152.7 6.8 %collective-permute-start.4 = (s32[4,8]{1,0:T(4,128)S(1)}, s32[4,8]{1,0:T(4,128)S(1)}, u32[]{:S(2)}, u32[]{:S(2)}) collective-permute-start(s32[4,8]{1,0:T(4,128)S(1)} %get-tuple-element.43), channel_id=1, source_target_pairs={{0,8},{8,16},{16,24},{24,32},{32,40},{40,48},{48,56},{56,64},{64,7... | collective-permute-start | bytes 392 | tf_op jit(solution)/shard_map/ppermute | solution.py:12
  156.7 4.9 %collective-permute-start.5 = (s32[4,8]{1,0:T(4,128)S(1)}, s32[4,8]{1,0:T(4,128)S(1)}, u32[]{:S(2)}, u32[]{:S(2)}) collective-permute-start(s32[4,8]{1,0:T(4,128)S(1)} %get-tuple-element.44), channel_id=1, source_target_pairs={{8,0},{16,8},{24,16},{32,24},{40,32},{48,40},{56,48},{64,56},{72,6... | collective-permute-start | bytes 392 | tf_op jit(solution)/shard_map/ppermute | solution.py:15
  161.7 4.2 %copy-start.7 = (bf16[1,16,8,128,128]{4,3,0,1,2:T(8,128)(2,1)S(1)}, bf16[1,16,8,128,128]{4,3,0,1,2:T(8,128)(2,1)}, u32[]{:S(2)}) copy-start(bf16[1,16,8,128,128]{4,3,0,1,2:T(8,128)(2,1)} %get-tuple-element.26) | copy-start | bytes 12582916
  161.7 7.6 %slice-start = ((s8[6291456]{0:T(1024)(128)(4,1)}), s8[4194304]{0:T(1024)(128)(4,1)S(1)}, s32[]{:S(2)}) async-start(s8[6291456]{0:T(1024)(128)(4,1)} %bitcast.472), calls=%async_computation.5 | async-start | bytes 8388608
  165.4 4.9 %slice-start.1 = ((s8[6291456]{0:T(1024)(128)(4,1)}), s8[2097152]{0:T(1024)(128)(4,1)S(1)}, s32[]{:S(2)}) async-start(s8[6291456]{0:T(1024)(128)(4,1)} %bitcast.472), calls=%async_computation.6 | async-start | bytes 4194304
  165.9 4.4 %copy-start.6 = (bf16[1,16,8,128,128]{4,3,0,1,2:T(8,128)(2,1)S(1)}, bf16[1,16,8,128,128]{4,3,0,1,2:T(8,128)(2,1)}, u32[]{:S(2)}) copy-start(bf16[1,16,8,128,128]{4,3,0,1,2:T(8,128)(2,1)} %get-tuple-element.29) | copy-start | bytes 12582916
  188.2 4.5 %copy-start.5 = (bf16[16,8,128,128]{3,2,0,1:T(8,128)(2,1)S(1)}, bf16[16,8,128,128]{3,2,0,1:T(8,128)(2,1)}, u32[]{:S(2)}) copy-start(bf16[16,8,128,128]{3,2,0,1:T(8,128)(2,1)} %get-tuple-element.24) | copy-start | bytes 12582916
  207.2 8.9 %copy-start.3 = (f32[16,128,8,128]{3,1,2,0:T(8,128)S(1)}, f32[16,128,8,128]{3,1,2,0:T(8,128)}, u32[]{:S(2)}) copy-start(f32[16,128,8,128]{3,1,2,0:T(8,128)} %fusion.20) | copy-start | bytes 25165828
  212.3 30.3 %collective-permute-start.6 = (bf16[2,4,8,128,128]{4,3,0,1,2:T(8,128)(2,1)}, bf16[2,4,8,128,128]{4,3,0,1,2:T(8,128)(2,1)S(1)}, u32[]{:S(2)}, u32[]{:S(2)}) collective-permute-start(bf16[2,4,8,128,128]{4,3,0,1,2:T(8,128)(2,1)} %get-tuple-element.42), channel_id=1, source_target_pairs={{0,8},{8,16},{16,24},{24,32},{32,40},{40,48},{48,56},{56,64},{64,7... | collective-permute-start | bytes 6291464 | tf_op jit(solution)/shard_map/ppermute | solution.py:12
  216.1 22.5 %copy-start.2 = (bf16[2,8,1024,128]{3,2,0,1:T(8,128)(2,1)S(1)}, bf16[2,8,1024,128]{3,2,0,1:T(8,128)(2,1)}, u32[]{:S(2)}) copy-start(bf16[2,8,1024,128]{3,2,0,1:T(8,128)(2,1)} %all-gather.6.cloned.1.call-done) | copy-start | bytes 12582916
  236.2 4.9 %copy-start.4 = (bf16[16,128,8,128]{3,1,2,0:T(8,128)(2,1)S(1)}, bf16[16,128,8,128]{3,1,2,0:T(8,128)(2,1)}, u32[]{:S(2)}) copy-start(bf16[16,128,8,128]{3,1,2,0:T(8,128)(2,1)} %select_convert_fusion) | copy-start | bytes 12582916
  236.2 27.8 %collective-permute-start.7 = (bf16[2,4,8,128,128]{4,3,0,1,2:T(8,128)(2,1)}, bf16[2,4,8,128,128]{4,3,0,1,2:T(8,128)(2,1)S(1)}, u32[]{:S(2)}, u32[]{:S(2)}) collective-permute-start(bf16[2,4,8,128,128]{4,3,0,1,2:T(8,128)(2,1)} %get-tuple-element.41), channel_id=1, source_target_pairs={{8,0},{16,8},{24,16},{32,24},{40,32},{48,40},{56,48},{64,56},{72,6... | collective-permute-start | bytes 6291464 | tf_op jit(solution)/shard_map/ppermute | solution.py:15
  265.8 1.0 copy-start.8
  267.3 0.8 copy-start.9
  319.3 12.6 %all-to-all-start.2 = ((f32[32,1,2,96]{3,2,1,0:T(2,128)}), f32[32,1,2,96]{3,2,1,0:T(2,128)S(1)}, u32[]{:S(2)}, u32[]{:S(2)}) async-start(f32[32,1,2,96]{3,2,1,0:T(2,128)} %broadcast_in_dim.170), calls=%async_computation.2 | async-start | bytes 65536 | tf_op jit(solution)/shard_map/all_to_all | solution.py:22
Sparse Core Ops, SparseCore 0:
  11.7 78.2 all-gather.3
  152.8 54.4 all-gather.5
where the time goes:
time: 343 us; the launch traced here: 342 us
  waiting for transfers between devices  126 us (37%)
  matrix products  69.8 us (20%)
  blocking collectives  47.2 us (14%)
  local copies, waits for them, and re-layouts  45.7 us (13%)
  starting transfers between devices  29 us (8%)
  between operations  15.5 us (5%)
  other arithmetic  8.87 us (3%)
    all_gather x1, waiting for transfers between devices, on_device(): whole_rows = lax.all_gather(stacked, 'orb', axis=2, tiled=True)  78.4 us
    dot_general x8, matrix products, all_slot_product(): jnp.matmul(factor_left[:, :, stride:stride + 1], source, preferred_elemen...  52.8 us
    all_to_all x2, blocking collectives, sent_to_all(): return lax.all_to_all(copies, axis, split_axis=0, concat_axis=0, tiled=True)  47.2 us
    ppermute x4, waiting for transfers between devices, padded_2(): lax.ppermute(lax.slice_in_dim(block, 0, width, axis=dim), axis, backward)  27.4 us
    ppermute x4, starting transfers between devices, padded_2(): lax.ppermute(lax.slice_in_dim(block, block.shape[dim] - width, None, axis...  15 us
    dot_general x32, matrix products, own_slot_product(): jnp.matmul(factor_left[:, :, stride], picked, preferred_element_type=jnp....  13.2 us
    unnamed x50, local copies, waits for them, and re-layouts  13.2 us
    slice x1, local copies, waits for them, and re-layouts, all_slot_product(): right_rims[:, stride:stride + count_rows]  11 us
  transfers between devices with their start and end apart: 11, of which 9 were waited for; matrix products, arithmetic and copies ran while one was open for 27% of the time, Pallas kernels for 0%

commit v1 on v0

v1 whole, which is shorter than its diff:
```python
import functools

import jax
import jax.numpy as jnp
from jax import lax
from jax.experimental import pallas as pl
from jax.experimental.pallas import tpu as pltpu
from jax.sharding import PartitionSpec as P

MESH = pl.DeviceIdType.MESH
BF16 = jnp.bfloat16
F32 = jnp.float32


def ring_kernel(
    sizes,
    pattern, fit_blocks, density_hbm, fields_hbm, tensor_hbm,
    out, sums,
    staged, keep_src, keep, win1, win2, lhs1, lhs2, result,
    integrals, piece, piece_x, piece_y, got_x, got_y, got_c, piece_f, part, parts_z,
    load_sem, in_send, in_recv, keep_send, keep_recv,
    fwd_send, fwd_recv, bwd_send, bwd_recv,
    out_send, out_recv,
    fx_send, fx_recv, fy_send, fy_recv, fc_send, fc_recv,
    z_send, z_recv, g_send, g_recv, h_send, h_recv,
):
    ys, xs, zs, rows, slots = sizes
    half = slots // 2
    blk = 128
    naux = ys * xs * 2
    total_rows = naux * rows
    aux = lax.axis_index("aux")
    z = lax.axis_index("orb")
    core = aux % 2
    col = aux // 2
    x = col % xs
    y = col // xs
    own_lo = half * blk

    def remote(src, dst, ss, rs, to_aux, to_z):
        return pltpu.make_async_remote_copy(
            src_ref=src, dst_ref=dst, send_sem=ss, recv_sem=rs,
            device_id={"aux": to_aux, "orb": to_z}, device_id_type=MESH,
        )

    def landed(ref, sem):
        pltpu.make_async_copy(ref, ref, sem).wait()

    row = col * (2 * zs) + 2 * z + core
    nxt = (row + 1) % total_rows
    prv = (row + total_rows - 1) % total_rows

    def holder(i):
        c = i // (2 * zs)
        q = i % (2 * zs)
        return 2 * c + q % 2, q // 2

    nxt_aux, nxt_z = holder(nxt)
    prv_aux, prv_z = holder(prv)

    load_d = pltpu.make_async_copy(density_hbm.at[:, 0], staged.at[0], load_sem.at[0])
    load_p = [
        pltpu.make_async_copy(fields_hbm.at[k, :, 0], staged.at[1 + k], load_sem.at[1 + k])
        for k in range(2)
    ]
    load_t = pltpu.make_async_copy(tensor_hbm, integrals, load_sem.at[3])
    load_d.start()
    load_p[0].start()
    load_p[1].start()
    load_t.start()

    barrier = pltpu.get_barrier_semaphore()
    greeted = 0

    def greet(a, b):
        pl.semaphore_signal(barrier, inc=1, device_id={"aux": a, "orb": b}, device_id_type=MESH)

    for step in range(1, zs):
        greet(aux, (z + step) % zs)
        greeted += 1
    for step in range(zs):
        greet(2 * col + 1 - core, (z + step) % zs)
        greeted += 1
    for step in range(1, 2 * xs):
        e = (2 * x + core + step) % (2 * xs)
        if xs > 1:
            @pl.when(e // 2 != x)
            def _():
                greet(2 * xs * y + e, z)
    greeted += 2 * (xs - 1)
    for step in range(1, ys):
        greet(2 * (((y + step) % ys) * xs + x) + core, z)
        greeted += 1
    at_top = (z == zs - 1) & (core == 1)
    at_bottom = (z == 0) & (core == 0)

    @pl.when(at_top)
    def _():
        greet(nxt_aux, nxt_z)

    @pl.when(at_bottom)
    def _():
        greet(prv_aux, prv_z)

    first_row = aux * rows
    column = first_row + z - half

    def mask_of(r):
        there = (pattern[r, z] == 1) & (column + r >= 0) & (column + r < total_rows)
        return jnp.where(there, 1, 0)

    for r in range(rows):
        keep_src[r] = jnp.full((8, blk), mask_of(r), jnp.int32)

    load_d.wait()
    for r in range(rows):
        factor = jnp.full((blk, blk), mask_of(r).astype(F32), F32).astype(BF16)
        staged[0, r] = staged[0, r] * factor

    pl.semaphore_wait(barrier, greeted + jnp.where(at_top | at_bottom, 1, 0))

    def dest_of(r):
        return 2 * col + r % 2, (zs // 2) * core + r // 2

    def send_in(mat, r):
        to_aux, to_z = dest_of(r)
        here = (to_aux == aux) & (to_z == z)
        dst = win1.at[mat, z, pl.ds(own_lo, blk)]

        @pl.when(here)
        def _():
            pltpu.make_async_copy(staged.at[mat, r], dst, in_recv.at[mat, z]).start()

        @pl.when(jnp.logical_not(here))
        def _():
            remote(staged.at[mat, r], dst, in_send.at[mat, r], in_recv.at[mat, z], to_aux, to_z).start()

    def send_keep(r):
        to_aux, to_z = dest_of(r)
        here = (to_aux == aux) & (to_z == z)

        @pl.when(here)
        def _():
            pltpu.make_async_copy(keep_src.at[r], keep.at[z], keep_recv.at[z]).start()

        @pl.when(jnp.logical_not(here))
        def _():
            remote(keep_src.at[r], keep.at[z], keep_send.at[r], keep_recv.at[z], to_aux, to_z).start()

    for r in range(rows):
        send_in(0, r)
    for k in range(2):
        load_p[k].wait()
        for r in range(rows):
            factor = jnp.full((blk, blk), mask_of(r).astype(F32), F32).astype(BF16)
            staged[1 + k, r] = staged[1 + k, r] * factor
        for r in range(rows):
            send_in(1 + k, r)
    for r in range(rows):
        send_keep(r)

    for t in range(slots):
        empty = range(t + half, slots) if t < half else range(0, t - half)
        for s in empty:
            for mat in range(3):
                win1[mat, s, pl.ds(t * blk, blk)] = jnp.zeros((blk, blk), BF16)
                win2[mat, s, pl.ds(t * blk, blk)] = jnp.zeros((blk, blk), BF16)

    def forward(win, phase, mat, step):
        t = half + 1 - step
        n = t + half - 1
        return remote(
            win.at[mat, pl.ds(1, n), pl.ds(t * blk, blk)],
            win.at[mat, pl.ds(0, n), pl.ds((t - 1) * blk, blk)],
            fwd_send.at[phase, mat, step - 1], fwd_recv.at[phase, mat, step - 1], nxt_aux, nxt_z,
        )

    def backward(win, phase, mat, step):
        t = half - 1 + step
        n = 2 * slots - half - 1 - t
        return remote(
            win.at[mat, pl.ds(t - half, n), pl.ds(t * blk, blk)],
            win.at[mat, pl.ds(t - half + 1, n), pl.ds((t + 1) * blk, blk)],
            bwd_send.at[phase, mat, step - 1], bwd_recv.at[phase, mat, step - 1], prv_aux, prv_z,
        )

    steps_f, steps_b = half, half - 1

    def advance(win, phase, mat, step):
        if step > 1 and step <= steps_f + 1:
            forward(win, phase, mat, step - 1).wait_recv()
        if step <= steps_f:
            forward(win, phase, mat, step).start()
        if step > 1 and step <= steps_b + 1:
            backward(win, phase, mat, step - 1).wait_recv()
        if step <= steps_b:
            backward(win, phase, mat, step).start()

    def arrived(mat):
        for u in range(slots):
            landed(win1.at[mat, u, pl.ds(own_lo, blk)], in_recv.at[mat, u])
        for u in range(slots):
            lhs1[mat, :, pl.ds(u * blk, blk)] = win1[mat, u, pl.ds(own_lo, blk)]

    def kept(s, value):
        mask = jnp.broadcast_to(keep[s, pl.ds(0, 1), :], (blk, blk))
        return jnp.where(mask > 0, value, 0.0)

    def square():
        def body(s, carry):
            value = jnp.dot(lhs1[0], win1[0, s], preferred_element_type=F32)
            win2[0, s, pl.ds(own_lo, blk)] = kept(s, value).astype(BF16)
            return carry

        lax.fori_loop(0, slots, body, 0)
        for s in range(slots):
            lhs2[0, :, pl.ds(s * blk, blk)] = win2[0, s, pl.ds(own_lo, blk)]

    def first(k):
        def body(s, carry):
            value = jnp.dot(lhs1[0], win1[1 + k, s], preferred_element_type=F32)
            value = value + jnp.dot(lhs1[1 + k], win1[0, s], preferred_element_type=F32)
            win2[1 + k, s, pl.ds(own_lo, blk)] = kept(s, value).astype(BF16)
            return carry

        lax.fori_loop(0, slots, body, 0)
        for s in range(slots):
            lhs2[1 + k, :, pl.ds(s * blk, blk)] = win2[1 + k, s, pl.ds(own_lo, blk)]

    def second(k):
        def body(s, carry):
            value = jnp.dot(lhs2[0], win2[1 + k, s], preferred_element_type=F32)
            value = value + jnp.dot(lhs2[1 + k], win2[0, s], preferred_element_type=F32)
            value = 2.0 * win2[1 + k, s, pl.ds(own_lo, blk)].astype(F32) - value
            result[k, s] = kept(s, value).astype(BF16)
            return carry

        lax.fori_loop(0, slots, body, 0)

    src_aux = 2 * col + z // (zs // 2)
    src_row = (2 * z + core) % rows

    def send_out(k, s):
        here = (src_aux == aux) & (z == s)
        dst = out.at[k, src_row, 0]

        @pl.when(here)
        def _():
            pltpu.make_async_copy(result.at[k, s], dst, out_recv.at[k, src_row]).start()

        @pl.when(jnp.logical_not(here))
        def _():
            remote(result.at[k, s], dst, out_send.at[k, s], out_recv.at[k, src_row], src_aux, s).start()

    done = steps_f + 1
    first_wave = (0, 1, 2, 5, 6, 7)
    for wave in range(first_wave[-1] + done):
        for item in range(6):
            step = wave - first_wave[item] + 1
            if step < 1 or step > done:
                continue
            phase, mat = item // 3, item % 3
            if step == 1 and phase == 0:
                arrived(mat)
            advance(win1 if phase == 0 else win2, phase, mat, step)
            if step == done and phase == 0:
                if mat == 0:
                    for u in range(slots):
                        landed(keep.at[u], keep_recv.at[u])
                    square()
                else:
                    first(mat - 1)
            if step == done and phase == 1 and mat > 0:
                second(mat - 1)
                for s in range(slots):
                    send_out(mat - 1, s)

    for k in range(2):
        for r in range(rows):
            landed(out.at[k, r, 0], out_recv.at[k, r])

    fitted = fit_blocks[0]
    owner = jnp.where(fitted // rows == aux, 1.0, 0.0)
    local_row = fitted % rows
    flag = jnp.full((blk, blk), owner, F32).astype(BF16)
    for k in range(2):
        piece[k] = out[k, local_row, 0] * flag

    def spread(src, got, ss, rs, count, target):
        copies = [
            remote(src, got.at[d - 1], ss.at[d - 1], rs.at[d - 1], target(d), z)
            for d in range(1, count)
        ]
        for c in copies:
            c.start()
        for c in copies:
            c.wait_recv()
        return copies

    pending = spread(
        piece, got_x, fx_send, fx_recv, xs, lambda d: 2 * (y * xs + (x + d) % xs) + core
    )
    for k in range(2):
        value = piece[k]
        for d in range(1, xs):
            value = value + got_x[d - 1, k]
        piece_x[k] = value
    pending += spread(
        piece_x, got_y, fy_send, fy_recv, ys, lambda d: 2 * (((y + d) % ys) * xs + x) + core
    )
    for k in range(2):
        value = piece_x[k]
        for d in range(1, ys):
            value = value + got_y[d - 1, k]
        piece_y[k] = value
    pending += spread(piece_y, got_c, fc_send, fc_recv, 2, lambda d: 2 * col + 1 - core)
    for k in range(2):
        piece_f[k] = (piece_y[k] + got_c[0, k]).astype(F32)

    load_t.wait()
    count_aux = integrals.shape[0]

    def contract(step, carry):
        acc0, acc1 = carry
        base = pl.multiple_of(step * 8, 8)
        rows0 = piece_f[0, pl.ds(base, 8)]
        rows1 = piece_f[1, pl.ds(base, 8)]
        for j in range(8):
            lanes = pl.ds(pl.multiple_of(step * 8 * blk + j * blk, blk), blk)
            slab = integrals[:, lanes].astype(F32)
            acc0 = acc0 + slab * rows0[j : j + 1]
            acc1 = acc1 + slab * rows1[j : j + 1]
        return acc0, acc1

    zero = jnp.zeros((count_aux, blk), F32)
    acc = lax.fori_loop(0, blk // 8, contract, (zero, zero))
    part[...] = jnp.zeros_like(part)
    for k in range(2):
        wide = jnp.concatenate([acc[k], jnp.zeros((blk - count_aux, blk), F32)], axis=0)
        part[pl.ds(k, 1)] = jnp.sum(wide.T, axis=0, keepdims=True)

    parts_z[z] = part[...]
    z_copies = [
        remote(part, parts_z.at[z], z_send.at[d - 1], z_recv.at[d - 1], aux, (z + d) % zs)
        for d in range(1, zs)
    ]
    for c in z_copies:
        c.start()
    for c in z_copies:
        c.wait_recv()
    total = parts_z[0]
    for d in range(1, zs):
        total = total + parts_z[d]
    sums[aux] = total

    group = 2 * xs
    e = 2 * x + core
    g_copies = [
        remote(sums.at[aux], sums.at[aux], g_send.at[d - 1], g_recv.at[d - 1], group * y + (e + d) % group, z)
        for d in range(1, group)
    ]
    for c in g_copies:
        c.start()
    for c in g_copies:
        c.wait_recv()
    mine = sums.at[pl.ds(group * y, group)]
    h_copies = [
        remote(mine, mine, h_send.at[d - 1], h_recv.at[d - 1], 2 * (((y + d) % ys) * xs + x) + core, z)
        for d in range(1, ys)
    ]
    for c in h_copies:
        c.start()
    for c in h_copies:
        c.wait_recv()

    for c in pending + z_copies + g_copies + h_copies:
        c.wait_send()
    for r in range(rows):
        to_aux, to_z = dest_of(r)

        @pl.when(jnp.logical_not((to_aux == aux) & (to_z == z)))
        def _():
            for mat in range(3):
                dst = win1.at[mat, z, pl.ds(own_lo, blk)]
                remote(staged.at[mat, r], dst, in_send.at[mat, r], in_recv.at[mat, z], to_aux, to_z).wait_send()
            remote(keep_src.at[r], keep.at[z], keep_send.at[r], keep_recv.at[z], to_aux, to_z).wait_send()
    for s in range(slots):
        @pl.when(jnp.logical_not((src_aux == aux) & (z == s)))
        def _():
            for k in range(2):
                remote(
                    result.at[k, s], out.at[k, src_row, 0], out_send.at[k, s], out_recv.at[k, src_row], src_aux, s
                ).wait_send()
    for phase, win in enumerate((win1, win2)):
        for mat in range(3):
            for step in range(1, steps_f + 1):
                forward(win, phase, mat, step).wait_send()
            for step in range(1, steps_b + 1):
                backward(win, phase, mat, step).wait_send()


def solution(mesh):
    naux, zs = mesh.shape["aux"], mesh.shape["orb"]
    side = {32: (4, 4), 8: (2, 2), 2: (1, 1)}[naux]
    ys, xs = side

    def on_device(band_pattern, density_in, field_terms, fit_blocks, tensor, metric_inv):
        rows = density_in.shape[0]
        slots = zs
        blk = density_in.shape[2]
        count_aux = tensor.shape[1]
        dma = pltpu.SemaphoreType.DMA
        vmem = pltpu.VMEM
        block = (blk, blk)
        half = slots // 2
        in_hbm = pl.BlockSpec(memory_space=pltpu.HBM)
        smem = pl.BlockSpec(memory_space=pltpu.SMEM)
        in_vmem = pl.BlockSpec(memory_space=pltpu.VMEM)
        response, sums = pl.pallas_call(
            functools.partial(ring_kernel, (ys, xs, zs, rows, slots)),
            out_shape=(
                jax.ShapeDtypeStruct(field_terms.shape, BF16),
                jax.ShapeDtypeStruct((naux, 8, blk), F32),
            ),
            in_specs=[smem, smem, in_hbm, in_hbm, in_hbm],
            out_specs=(in_vmem, in_vmem),
            scratch_shapes=[
                vmem((3, rows, *block), BF16),
                vmem((rows, 8, blk), jnp.int32),
                vmem((slots, 8, blk), jnp.int32),
                vmem((3, slots, slots * blk, blk), BF16),
                vmem((3, slots, slots * blk, blk), BF16),
                vmem((3, blk, slots * blk), BF16),
                vmem((3, blk, slots * blk), BF16),
                vmem((2, slots, *block), BF16),
                vmem((count_aux, blk * blk), BF16),
                vmem((2, *block), BF16),
                vmem((2, *block), BF16),
                vmem((2, *block), BF16),
                vmem((max(xs - 1, 1), 2, *block), BF16),
                vmem((max(ys - 1, 1), 2, *block), BF16),
                vmem((1, 2, *block), BF16),
                vmem((2, *block), F32),
                vmem((8, blk), F32),
                vmem((zs, 8, blk), F32),
                dma((4,)),
                dma((3, rows)), dma((3, slots)),
                dma((rows,)), dma((slots,)),
                dma((2, 3, half)), dma((2, 3, half)),
                dma((2, 3, half)), dma((2, 3, half)),
                dma((2, slots)), dma((2, rows)),
                dma((max(xs - 1, 1),)), dma((max(xs - 1, 1),)),
                dma((max(ys - 1, 1),)), dma((max(ys - 1, 1),)),
                dma((1,)), dma((1,)),
                dma((zs,)), dma((zs,)),
                dma((2 * xs,)), dma((2 * xs,)),
                dma((max(ys - 1, 1),)), dma((max(ys - 1, 1),)),
            ],
            compiler_params=pltpu.CompilerParams(
                collective_id=0, has_side_effects=True, vmem_limit_bytes=48 << 20
            ),
        )(
            band_pattern, fit_blocks, density_in, field_terms,
            tensor.reshape(count_aux, blk * blk),
        )
        full = sums[:, :2, :count_aux].transpose(1, 0, 2).reshape(1, 2, naux * count_aux)
        coefficients = jnp.einsum("fpq,fkq->fkp", metric_inv, full, precision=lax.Precision.HIGHEST)
        return response, coefficients

    in_specs = (
        P("aux", None),
        P("aux", "orb", None, None),
        P(None, "aux", "orb", None, None),
        P(),
        P(None, "aux", "orb", None),
        P(None, "aux", None),
    )
    out_specs = (P(None, "aux", "orb", None, None), P(None, None, "aux"))
    return jax.shard_map(
        on_device, mesh=mesh, in_specs=in_specs, out_specs=out_specs, check_vma=False
    )
```

time: 343 us -> 149 us (0.43)
  Pallas kernels: 0 us -> 141 us
  waiting for transfers between devices: 126 us -> 0 us
  matrix products: 69.8 us -> 1.59 us
  blocking collectives: 47.2 us -> 0 us
  local copies, waits for them, and re-layouts: 45.7 us -> 5.47 us
  starting transfers between devices: 29 us -> 0 us
  between operations: 15.5 us -> 1.43 us
  other arithmetic: 8.87 us -> 0 us
    pallas_call x0 -> x1, Pallas kernels: none -> 141 us  [on_device(): pl.pallas_call(functools.partial(ring_kernel, (ys, xs, zs, rows, slots)),...]
    all_gather x2 -> x0, waiting for transfers between devices: 82.6 us -> none  [the longest x1 78.4 us: on_device(): whole_rows = lax.all_gather(stacked, 'orb', axis=2, tiled=True)]
    dot_general x42 -> x1, matrix products: 69.8 us -> 1.59 us  [on_device(): jnp.einsum('fpq,fkq->fkp', metric_inv, full, precision=lax.Precision.HIGH...]
    all_to_all x2 -> x0, blocking collectives: 47.2 us -> none  [sent_to_all(): return lax.all_to_all(copies, axis, split_axis=0, concat_axis=0, tiled=True)]
    ppermute x8 -> x0, waiting for transfers between devices: 37.6 us -> none  [the longest x4 27.4 us: padded_2(): lax.ppermute(lax.slice_in_dim(block, 0, width, axis=dim), axis, backward)]
    ppermute x8 -> x0, starting transfers between devices: 23.6 us -> none  [the longest x4 15 us: padded_2(): lax.ppermute(lax.slice_in_dim(block, block.shape[dim] - width, None, axis...]
    slice x5 -> x0, local copies, waits for them, and re-layouts: 20.8 us -> none  [the longest x1 11 us: all_slot_product(): right_rims[:, stride:stride + count_rows]]
    unnamed x50 -> x11, local copies, waits for them, and re-layouts: 13.2 us -> 5.36 us
  transfers between devices with their start and end apart: 11 -> 0, of which waited for: 9 -> 0; matrix products, arithmetic and copies ran while one was open for 27% -> 0% of each run, Pallas kernels for 0% -> 0%
where the time goes in v1:
time: 149 us
  Pallas kernels  141 us (95%)
  local copies, waits for them, and re-layouts  5.47 us (4%)
  matrix products  1.59 us (1%)
    pallas_call x1, Pallas kernels, on_device(): pl.pallas_call(functools.partial(ring_kernel, (ys, xs, zs, rows, slots)),...  141 us
    unnamed x11, local copies, waits for them, and re-layouts  5.36 us

profile of v1, /device:TPU:1, one launch (start us, length us, event | category | flops | bytes accessed | tf_op | source)
XLA Modules:
  0.0 149.0 jit_solution(11114170501587697593)
XLA Ops:
  0.6 0.0 copy-start
  1.4 0.0 copy-start.1
  1.4 1.9 %copy-done.1 = bf16[1,96,1,16384]{3,1,2,0:T(8,128)(2,1)S(1)} copy-done((bf16[1,96,1,16384]{3,1,2,0:T(8,128)(2,1)S(1)}, bf16[1,96,1,16384]{3,1,2,0:T(8,128)(2,1)}, u32[]{:S(2)}) %copy-start.1) | copy-done | bytes 3145752
  3.3 0.0 copy-start.2
  3.3 1.0 copy-done.2
  4.3 0.0 copy-start.3
  4.3 0.9 copy-done.3
  5.3 0.0 copy-start.4
  5.3 0.7 copy-done.4
  6.0 140.5 %shard_map.77 = (bf16[2,8,1,128,128]{4,3,2,1,0:T(8,128)(2,1)S(1)}, f32[32,8,128]{2,1,0:T(8,128)S(1)}) custom-call(s32[8,8]{1,0:T(8,128)S(1)} %copy-done.4, s32[1]{0:T(128)S(6)} %copy.10.fit_blocks, bf16[8,1,128,128]{3,2,1,0:T(8,128)(2,1)S(1)} %copy-done.3, bf16[2,8,1,128,128]{4,3,2,1,0:T(8,128)(2,1)S(1)} %copy-done.2, bf16[96,16384]{1,0:T(8,128)(2,1)S(1)} %bitcast.11), custom_call_target="tpu_custom_call" | custom-call | tf_op jit(solution)/shard_map/pallas_call | solution.py:419
  146.5 0.1 reshape.17
  146.6 0.0 copy-done
  146.6 1.6 %fusion.2 = f32[1,2,96]{2,1,0:T(2,128)} fusion(f32[2,3072]{1,0:T(2,128)S(1)} %reshape.17, f32[1,96,3072]{2,1,0:T(8,128)S(1)} %copy-done), kind=kOutput, calls=%fused_computation.2 | convolution fusion | flops 7077888 | bytes 1204992 | tf_op jit(solution)/shard_map/fpq,fkq->fkp/dot_general | solution.py:467
  148.2 0.8 copy.11
  (2 shorter events, 0.0 us)
Async XLA Ops:
  0.6 146.0 %copy-start = (f32[1,96,3072]{2,1,0:T(8,128)S(1)}, f32[1,96,3072]{2,1,0:T(8,128)}, u32[]{:S(2)}) copy-start(f32[1,96,3072]{2,1,0:T(8,128)} %param.11) | copy-start | bytes 3538948
  1.4 1.9 %copy-start.1 = (bf16[1,96,1,16384]{3,1,2,0:T(8,128)(2,1)S(1)}, bf16[1,96,1,16384]{3,1,2,0:T(8,128)(2,1)}, u32[]{:S(2)}) copy-start(bf16[1,96,1,16384]{3,1,2,0:T(8,128)(2,1)} %param.10) | copy-start | bytes 9437188
  3.3 1.0 copy-start.2
  4.3 0.9 copy-start.3
  5.3 0.7 copy-start.4

commit v2 on v1

--- a/solution.py
+++ b/solution.py
@@ -19,7 +19,7 @@
     staged, keep_src, keep, win1, win2, lhs1, lhs2, result,
     integrals, piece, piece_x, piece_y, got_x, got_y, got_c, piece_f, part, parts_z,
     load_sem, in_send, in_recv, keep_send, keep_recv,
-    fwd_send, fwd_recv, bwd_send, bwd_recv,
+    win_send, win_recv,
     out_send, out_recv,
     fx_send, fx_recv, fy_send, fy_recv, fc_send, fc_recv,
     z_send, z_recv, g_send, g_recv, h_send, h_recv,
@@ -46,17 +46,17 @@
     def landed(ref, sem):
         pltpu.make_async_copy(ref, ref, sem).wait()
 
-    row = col * (2 * zs) + 2 * z + core
-    nxt = (row + 1) % total_rows
-    prv = (row + total_rows - 1) % total_rows
+    row = 2 * xs * zs * y + 2 * (z * xs + x) + core
 
     def holder(i):
-        c = i // (2 * zs)
-        q = i % (2 * zs)
-        return 2 * c + q % 2, q // 2
-
-    nxt_aux, nxt_z = holder(nxt)
-    prv_aux, prv_z = holder(prv)
+        i = (i + total_rows) % total_rows
+        pair = (i % (2 * xs * zs)) // 2
+        return 2 * (i // (2 * xs * zs) * xs + pair % xs) + i % 2, pair // xs
+
+    def dest_of(r):
+        return holder(aux * rows + r)
+
+    src_aux, src_row = row // rows, row % rows
 
     load_d = pltpu.make_async_copy(density_hbm.at[:, 0], staged.at[0], load_sem.at[0])
     load_p = [
@@ -75,32 +75,32 @@
     def greet(a, b):
         pl.semaphore_signal(barrier, inc=1, device_id={"aux": a, "orb": b}, device_id_type=MESH)
 
+    self_holds = src_aux == aux
+    for r in range(rows):
+        to_aux, to_z = dest_of(r)
+
+        @pl.when(jnp.logical_not((to_aux == aux) & (to_z == z)))
+        def _():
+            greet(to_aux, to_z)
+
+    for s in range(zs):
+        @pl.when(jnp.logical_not((src_aux == aux) & (z == s)))
+        def _():
+            greet(src_aux, s)
+
+    greeted += rows + zs
+    for offset in (-2, -1, 1, 2):
+        greet(*holder(row + offset))
+    greeted += 4
     for step in range(1, zs):
         greet(aux, (z + step) % zs)
-        greeted += 1
-    for step in range(zs):
-        greet(2 * col + 1 - core, (z + step) % zs)
-        greeted += 1
+    greeted += zs - 1
     for step in range(1, 2 * xs):
-        e = (2 * x + core + step) % (2 * xs)
-        if xs > 1:
-            @pl.when(e // 2 != x)
-            def _():
-                greet(2 * xs * y + e, z)
-    greeted += 2 * (xs - 1)
+        greet(2 * xs * y + (2 * x + core + step) % (2 * xs), z)
+    greeted += 2 * xs - 1
     for step in range(1, ys):
         greet(2 * (((y + step) % ys) * xs + x) + core, z)
         greeted += 1
-    at_top = (z == zs - 1) & (core == 1)
-    at_bottom = (z == 0) & (core == 0)
-
-    @pl.when(at_top)
-    def _():
-        greet(nxt_aux, nxt_z)
-
-    @pl.when(at_bottom)
-    def _():
-        greet(prv_aux, prv_z)
 
     first_row = aux * rows
     column = first_row + z - half
@@ -117,10 +117,7 @@
         factor = jnp.full((blk, blk), mask_of(r).astype(F32), F32).astype(BF16)
         staged[0, r] = staged[0, r] * factor
 
-    pl.semaphore_wait(barrier, greeted + jnp.where(at_top | at_bottom, 1, 0))
-
-    def dest_of(r):
-        return 2 * col + r % 2, (zs // 2) * core + r // 2
+    pl.semaphore_wait(barrier, greeted - jnp.where(self_holds, 2, 0))
 
     def send_in(mat, r):
         to_aux, to_z = dest_of(r)
@@ -149,6 +146,8 @@
 
     for r in range(rows):
         send_in(0, r)
+    for r in range(rows):
+        send_keep(r)
     for k in range(2):
         load_p[k].wait()
         for r in range(rows):
@@ -156,8 +155,6 @@
             staged[1 + k, r] = staged[1 + k, r] * factor
         for r in range(rows):
             send_in(1 + k, r)
-    for r in range(rows):
-        send_keep(r)
 
     for t in range(slots):
         empty = range(t + half, slots) if t < half else range(0, t - half)
@@ -166,35 +163,49 @@
                 win1[mat, s, pl.ds(t * blk, blk)] = jnp.zeros((blk, blk), BF16)
                 win2[mat, s, pl.ds(t * blk, blk)] = jnp.zeros((blk, blk), BF16)
 
-    def forward(win, phase, mat, step):
-        t = half + 1 - step
-        n = t + half - 1
+    def slots_of(t):
+        return max(0, t - half), min(slots, t + half)
+
+    def message(win, phase, mat, index, t, offset):
+        to = t - offset
+        lo, hi = slots_of(to)
+        to_aux, to_z = holder(row + offset)
         return remote(
-            win.at[mat, pl.ds(1, n), pl.ds(t * blk, blk)],
-            win.at[mat, pl.ds(0, n), pl.ds((t - 1) * blk, blk)],
-            fwd_send.at[phase, mat, step - 1], fwd_recv.at[phase, mat, step - 1], nxt_aux, nxt_z,
+            win.at[mat, pl.ds(lo + offset, hi - lo), pl.ds(t * blk, blk)],
+            win.at[mat, pl.ds(lo, hi - lo), pl.ds(to * blk, blk)],
+            win_send.at[phase, mat, index], win_recv.at[phase, mat, to], to_aux, to_z,
         )
 
-    def backward(win, phase, mat, step):
-        t = half - 1 + step
-        n = 2 * slots - half - 1 - t
-        return remote(
-            win.at[mat, pl.ds(t - half, n), pl.ds(t * blk, blk)],
-            win.at[mat, pl.ds(t - half + 1, n), pl.ds((t + 1) * blk, blk)],
-            bwd_send.at[phase, mat, step - 1], bwd_recv.at[phase, mat, step - 1], prv_aux, prv_z,
-        )
-
-    steps_f, steps_b = half, half - 1
+    def got(win, phase, mat, t):
+        lo, hi = slots_of(t)
+        landed(win.at[mat, pl.ds(lo, hi - lo), pl.ds(t * blk, blk)], win_recv.at[phase, mat, t])
+
+    plan = (
+        (
+            ((), ((half, 2), (half, -1), (half, 1))),
+            ((3, 2), ((3, 2), (2, 2), (3, 1), (2, 1))),
+            ((1, 0), ((1, 1),)),
+            ((5, 6, 7), ()),
+        ),
+        (
+            ((), ((half, 1), (half, -2), (half, -1))),
+            ((5, 6), ((5, -2), (5, -1), (6, -1))),
+            ((7,), ()),
+            ((3, 2, 1, 0), ()),
+        ),
+    )
 
     def advance(win, phase, mat, step):
-        if step > 1 and step <= steps_f + 1:
-            forward(win, phase, mat, step - 1).wait_recv()
-        if step <= steps_f:
-            forward(win, phase, mat, step).start()
-        if step > 1 and step <= steps_b + 1:
-            backward(win, phase, mat, step - 1).wait_recv()
-        if step <= steps_b:
-            backward(win, phase, mat, step).start()
+        for c in range(2):
+            @pl.when(core == c)
+            def _():
+                waits, sends = plan[c][step - 1]
+                index = sum(len(plan[c][j][1]) for j in range(step - 1))
+                for t in waits:
+                    got(win, phase, mat, t)
+                for t, offset in sends:
+                    message(win, phase, mat, index, t, offset).start()
+                    index += 1
 
     def arrived(mat):
         for u in range(slots):
@@ -237,9 +248,6 @@
 
         lax.fori_loop(0, slots, body, 0)
 
-    src_aux = 2 * col + z // (zs // 2)
-    src_row = (2 * z + core) % rows
-
     def send_out(k, s):
         here = (src_aux == aux) & (z == s)
         dst = out.at[k, src_row, 0]
@@ -252,8 +260,8 @@
         def _():
             remote(result.at[k, s], dst, out_send.at[k, s], out_recv.at[k, src_row], src_aux, s).start()
 
-    done = steps_f + 1
-    first_wave = (0, 1, 2, 5, 6, 7)
+    done = 4
+    first_wave = (0, 1, 2, 3, 4, 5)
     for wave in range(first_wave[-1] + done):
         for item in range(6):
             step = wave - first_wave[item] + 1
@@ -262,14 +270,14 @@
             phase, mat = item // 3, item % 3
             if step == 1 and phase == 0:
                 arrived(mat)
-            advance(win1 if phase == 0 else win2, phase, mat, step)
-            if step == done and phase == 0:
+            if step == 1 and phase == 1:
                 if mat == 0:
                     for u in range(slots):
                         landed(keep.at[u], keep_recv.at[u])
                     square()
                 else:
                     first(mat - 1)
+            advance(win1 if phase == 0 else win2, phase, mat, step)
             if step == done and phase == 1 and mat > 0:
                 second(mat - 1)
                 for s in range(slots):
@@ -286,36 +294,43 @@
     for k in range(2):
         piece[k] = out[k, local_row, 0] * flag
 
-    def spread(src, got, ss, rs, count, target):
+    def over_x(d):
+        return 2 * (y * xs + (x + d) % xs) + core
+
+    def over_y(d):
+        return 2 * (((y + d) % ys) * xs + x) + core
+
+    pending = []
+
+    def spread(src, got_there, count, ss, rs, target):
         copies = [
-            remote(src, got.at[d - 1], ss.at[d - 1], rs.at[d - 1], target(d), z)
+            remote(src, got_there.at[d - 1], ss.at[d - 1], rs.at[d - 1], target(d), z)
             for d in range(1, count)
         ]
         for c in copies:
             c.start()
-        for c in copies:
+        pending.extend(copies)
+        return copies
+
+    def added(src, got_there, copies):
+        value = src[...]
+        for d, c in enumerate(copies):
             c.wait_recv()
-        return copies
-
-    pending = spread(
-        piece, got_x, fx_send, fx_recv, xs, lambda d: 2 * (y * xs + (x + d) % xs) + core
-    )
-    for k in range(2):
-        value = piece[k]
-        for d in range(1, xs):
-            value = value + got_x[d - 1, k]
-        piece_x[k] = value
-    pending += spread(
-        piece_x, got_y, fy_send, fy_recv, ys, lambda d: 2 * (((y + d) % ys) * xs + x) + core
-    )
-    for k in range(2):
-        value = piece_x[k]
-        for d in range(1, ys):
-            value = value + got_y[d - 1, k]
-        piece_y[k] = value
-    pending += spread(piece_y, got_c, fc_send, fc_recv, 2, lambda d: 2 * col + 1 - core)
-    for k in range(2):
-        piece_f[k] = (piece_y[k] + got_c[0, k]).astype(F32)
+            value = value + got_there[d]
+        return value
+
+    first_x = spread(piece.at[0], got_x.at[0], xs, fx_send.at[0], fx_recv.at[0], over_x)
+    first_y = spread(piece.at[1], got_y.at[0], ys, fy_send.at[0], fy_recv.at[0], over_y)
+    piece_x[0] = added(piece.at[0], got_x.at[0], first_x)
+    then_y = spread(piece_x.at[0], got_y.at[1], ys, fy_send.at[1], fy_recv.at[1], over_y)
+    piece_x[1] = added(piece.at[1], got_y.at[0], first_y)
+    then_x = spread(piece_x.at[1], got_x.at[1], xs, fx_send.at[1], fx_recv.at[1], over_x)
+    piece_y[0] = added(piece_x.at[0], got_y.at[1], then_y)
+    over0 = spread(piece_y.at[0], got_c.at[0], 2, fc_send.at[0], fc_recv.at[0], lambda d: aux + 1 - 2 * core)
+    piece_y[1] = added(piece_x.at[1], got_x.at[1], then_x)
+    over1 = spread(piece_y.at[1], got_c.at[1], 2, fc_send.at[1], fc_recv.at[1], lambda d: aux + 1 - 2 * core)
+    piece_f[0] = added(piece_y.at[0], got_c.at[0], over0).astype(F32)
+    piece_f[1] = added(piece_y.at[1], got_c.at[1], over1).astype(F32)
 
     load_t.wait()
     count_aux = integrals.shape[0]
@@ -391,17 +406,19 @@
                 remote(
                     result.at[k, s], out.at[k, src_row, 0], out_send.at[k, s], out_recv.at[k, src_row], src_aux, s
                 ).wait_send()
-    for phase, win in enumerate((win1, win2)):
-        for mat in range(3):
-            for step in range(1, steps_f + 1):
-                forward(win, phase, mat, step).wait_send()
-            for step in range(1, steps_b + 1):
-                backward(win, phase, mat, step).wait_send()
+    for c in range(2):
+        @pl.when(core == c)
+        def _():
+            sends = [one for stage in plan[c] for one in stage[1]]
+            for phase, win in enumerate((win1, win2)):
+                for mat in range(3):
+                    for index, (t, offset) in enumerate(sends):
+                        message(win, phase, mat, index, t, offset).wait_send()
 
 
 def solution(mesh):
     naux, zs = mesh.shape["aux"], mesh.shape["orb"]
-    side = {32: (4, 4), 8: (2, 2), 2: (1, 1)}[naux]
+    side = {32: (4, 4), 8: (2, 2), 4: (1, 2), 2: (1, 1)}[naux]
     ys, xs = side
 
     def on_device(band_pattern, density_in, field_terms, fit_blocks, tensor, metric_inv):
@@ -412,7 +429,6 @@
         dma = pltpu.SemaphoreType.DMA
         vmem = pltpu.VMEM
         block = (blk, blk)
-        half = slots // 2
         in_hbm = pl.BlockSpec(memory_space=pltpu.HBM)
         smem = pl.BlockSpec(memory_space=pltpu.SMEM)
         in_vmem = pl.BlockSpec(memory_space=pltpu.VMEM)
@@ -437,27 +453,26 @@
                 vmem((2, *block), BF16),
                 vmem((2, *block), BF16),
                 vmem((2, *block), BF16),
-                vmem((max(xs - 1, 1), 2, *block), BF16),
-                vmem((max(ys - 1, 1), 2, *block), BF16),
-                vmem((1, 2, *block), BF16),
+                vmem((2, max(xs - 1, 1), *block), BF16),
+                vmem((2, max(ys - 1, 1), *block), BF16),
+                vmem((2, 1, *block), BF16),
                 vmem((2, *block), F32),
                 vmem((8, blk), F32),
                 vmem((zs, 8, blk), F32),
                 dma((4,)),
                 dma((3, rows)), dma((3, slots)),
                 dma((rows,)), dma((slots,)),
-                dma((2, 3, half)), dma((2, 3, half)),
-                dma((2, 3, half)), dma((2, 3, half)),
+                dma((2, 3, slots)), dma((2, 3, slots)),
                 dma((2, slots)), dma((2, rows)),
-                dma((max(xs - 1, 1),)), dma((max(xs - 1, 1),)),
-                dma((max(ys - 1, 1),)), dma((max(ys - 1, 1),)),
-                dma((1,)), dma((1,)),
+                dma((2, max(xs - 1, 1))), dma((2, max(xs - 1, 1))),
+                dma((2, max(ys - 1, 1))), dma((2, max(ys - 1, 1))),
+                dma((2, 1)), dma((2, 1)),
                 dma((zs,)), dma((zs,)),
                 dma((2 * xs,)), dma((2 * xs,)),
                 dma((max(ys - 1, 1),)), dma((max(ys - 1, 1),)),
             ],
             compiler_params=pltpu.CompilerParams(
-                collective_id=0, has_side_effects=True, vmem_limit_bytes=48 << 20
+                collective_id=0, has_side_effects=True, vmem_limit_bytes=62 << 20
             ),
         )(
             band_pattern, fit_blocks, density_in, field_terms,

time: 149 us -> 170 us (1.14)
  Pallas kernels: 141 us -> 165 us
  local copies, waits for them, and re-layouts: 5.47 us -> 1.88 us
    pallas_call x1, Pallas kernels: 141 us -> 165 us  [on_device(): pl.pallas_call(functools.partial(ring_kernel, (ys, xs, zs, rows, slots)),...]
    unnamed x11 -> x5, local copies, waits for them, and re-layouts: 5.36 us -> 0.81 us
where the time goes in v2:
time: 170 us
  Pallas kernels  165 us (97%)
  local copies, waits for them, and re-layouts  1.88 us (1%)
    pallas_call x1, Pallas kernels, on_device(): pl.pallas_call(functools.partial(ring_kernel, (ys, xs, zs, rows, slots)),...  165 us

profile of v2, /device:TPU:1, one launch (start us, length us, event | category | flops | bytes accessed | tf_op | source)
XLA Modules:
  0.0 169.8 jit_solution(18029344142190618090)
XLA Ops:
  0.6 0.0 copy-start
  1.4 164.9 %shard_map.77 = (bf16[2,8,1,128,128]{4,3,2,1,0:T(8,128)(2,1)}, f32[32,8,128]{2,1,0:T(8,128)}) custom-call(s32[8,8]{1,0:T(8,128)} %pattern.1, s32[1]{0:T(128)S(6)} %copy.10.fit_blocks, bf16[8,1,128,128]{3,2,1,0:T(8,128)(2,1)} %density_hbm.1, bf16[2,8,1,128,128]{4,3,2,1,0:T(8,128)(2,1)} %fields_hbm.1, bf16[96,16384]{1,0:T(8,128)(2,1)} %bitcast.11), custom_call_target="tpu_custom_call" | custom-call | tf_op jit(solution)/shard_map/pallas_call | solution.py:435
  166.3 0.0 copy-start.1
  166.3 1.0 slice_bitcast_fusion
  167.3 0.1 reshape.17
  167.4 0.0 copy-done
  167.4 1.6 fusion.2
  169.0 0.0 copy-done.1
  169.0 0.8 copy.11
  (1 shorter events, 0.0 us)
Async XLA Ops:
  0.6 166.7 %copy-start = (f32[1,96,3072]{2,1,0:T(8,128)S(1)}, f32[1,96,3072]{2,1,0:T(8,128)}, u32[]{:S(2)}) copy-start(f32[1,96,3072]{2,1,0:T(8,128)} %param.11) | copy-start | bytes 3538948
  166.3 2.7 %copy-start.1 = (bf16[2,8,1,128,128]{4,3,2,1,0:T(8,128)(2,1)S(1)}, bf16[2,8,1,128,128]{4,3,2,1,0:T(8,128)(2,1)}, u32[]{:S(2)}) copy-start(bf16[2,8,1,128,128]{4,3,2,1,0:T(8,128)(2,1)} %get-tuple-element.8) | copy-start | bytes 1572868

commit v3 on v2

--- a/solution.py
+++ b/solution.py
@@ -14,8 +14,8 @@
 
 def ring_kernel(
     sizes,
-    pattern, fit_blocks, density_hbm, fields_hbm, tensor_hbm,
-    out, sums,
+    pattern, fit_blocks, density_hbm, fields_hbm, tensor_hbm, metric_hbm,
+    out, coefficients, sums, metric,
     staged, keep_src, keep, win1, win2, lhs1, lhs2, result,
     integrals, piece, piece_x, piece_y, got_x, got_y, got_c, piece_f, part, parts_z,
     load_sem, in_send, in_recv, keep_send, keep_recv,
@@ -46,12 +46,13 @@
     def landed(ref, sem):
         pltpu.make_async_copy(ref, ref, sem).wait()
 
-    row = 2 * xs * zs * y + 2 * (z * xs + x) + core
+    row = 2 * zs * col + 2 * (z + col % 2 * (zs - 1 - 2 * z)) + core
 
     def holder(i):
         i = (i + total_rows) % total_rows
-        pair = (i % (2 * xs * zs)) // 2
-        return 2 * (i // (2 * xs * zs) * xs + pair % xs) + i % 2, pair // xs
+        q = (i % (2 * zs)) // 2
+        c = i // (2 * zs)
+        return 2 * c + i % 2, q + c % 2 * (zs - 1 - 2 * q)
 
     def dest_of(r):
         return holder(aux * rows + r)
@@ -68,6 +69,8 @@
     load_p[0].start()
     load_p[1].start()
     load_t.start()
+    load_m = pltpu.make_async_copy(metric_hbm.at[0], metric, load_sem.at[4])
+    load_m.start()
 
     barrier = pltpu.get_barrier_semaphore()
     greeted = 0
@@ -238,27 +241,28 @@
         for s in range(slots):
             lhs2[1 + k, :, pl.ds(s * blk, blk)] = win2[1 + k, s, pl.ds(own_lo, blk)]
 
+    def send_out(k, s):
+        here = (src_aux == aux) & (z == s)
+        dst = out.at[k, src_row, 0]
+
+        @pl.when(here)
+        def _():
+            pltpu.make_async_copy(result.at[k, s], dst, out_recv.at[k, src_row]).start()
+
+        @pl.when(jnp.logical_not(here))
+        def _():
+            remote(result.at[k, s], dst, out_send.at[k, s], out_recv.at[k, src_row], src_aux, s).start()
+
     def second(k):
         def body(s, carry):
             value = jnp.dot(lhs2[0], win2[1 + k, s], preferred_element_type=F32)
             value = value + jnp.dot(lhs2[1 + k], win2[0, s], preferred_element_type=F32)
             value = 2.0 * win2[1 + k, s, pl.ds(own_lo, blk)].astype(F32) - value
             result[k, s] = kept(s, value).astype(BF16)
+            send_out(k, s)
             return carry
 
         lax.fori_loop(0, slots, body, 0)
-
-    def send_out(k, s):
-        here = (src_aux == aux) & (z == s)
-        dst = out.at[k, src_row, 0]
-
-        @pl.when(here)
-        def _():
-            pltpu.make_async_copy(result.at[k, s], dst, out_recv.at[k, src_row]).start()
-
-        @pl.when(jnp.logical_not(here))
-        def _():
-            remote(result.at[k, s], dst, out_send.at[k, s], out_recv.at[k, src_row], src_aux, s).start()
 
     done = 4
     first_wave = (0, 1, 2, 3, 4, 5)
@@ -280,19 +284,8 @@
             advance(win1 if phase == 0 else win2, phase, mat, step)
             if step == done and phase == 1 and mat > 0:
                 second(mat - 1)
-                for s in range(slots):
-                    send_out(mat - 1, s)
-
-    for k in range(2):
-        for r in range(rows):
-            landed(out.at[k, r, 0], out_recv.at[k, r])
 
     fitted = fit_blocks[0]
-    owner = jnp.where(fitted // rows == aux, 1.0, 0.0)
-    local_row = fitted % rows
-    flag = jnp.full((blk, blk), owner, F32).astype(BF16)
-    for k in range(2):
-        piece[k] = out[k, local_row, 0] * flag
 
     def over_x(d):
         return 2 * (y * xs + (x + d) % xs) + core
@@ -319,40 +312,57 @@
             value = value + got_there[d]
         return value
 
-    first_x = spread(piece.at[0], got_x.at[0], xs, fx_send.at[0], fx_recv.at[0], over_x)
-    first_y = spread(piece.at[1], got_y.at[0], ys, fy_send.at[0], fy_recv.at[0], over_y)
-    piece_x[0] = added(piece.at[0], got_x.at[0], first_x)
-    then_y = spread(piece_x.at[0], got_y.at[1], ys, fy_send.at[1], fy_recv.at[1], over_y)
-    piece_x[1] = added(piece.at[1], got_y.at[0], first_y)
-    then_x = spread(piece_x.at[1], got_x.at[1], xs, fx_send.at[1], fx_recv.at[1], over_x)
-    piece_y[0] = added(piece_x.at[0], got_y.at[1], then_y)
-    over0 = spread(piece_y.at[0], got_c.at[0], 2, fc_send.at[0], fc_recv.at[0], lambda d: aux + 1 - 2 * core)
-    piece_y[1] = added(piece_x.at[1], got_x.at[1], then_x)
-    over1 = spread(piece_y.at[1], got_c.at[1], 2, fc_send.at[1], fc_recv.at[1], lambda d: aux + 1 - 2 * core)
-    piece_f[0] = added(piece_y.at[0], got_c.at[0], over0).astype(F32)
-    piece_f[1] = added(piece_y.at[1], got_c.at[1], over1).astype(F32)
-
+    def piece_of(k):
+        for r in range(rows):
+            landed(out.at[k, r, 0], out_recv.at[k, r])
+        value = jnp.zeros((blk, blk), BF16)
+        for r in range(rows):
+            chosen = jnp.where(fitted == first_row + r, 1.0, 0.0)
+            value = value + out[k, r, 0] * jnp.full((blk, blk), chosen, F32).astype(BF16)
+        piece[k] = value
+
+    def other_core(d):
+        return aux + 1 - 2 * core
+
+    count_aux = integrals.shape[0]
+
+    def contract(k):
+        def body(step, acc):
+            rows_of = piece_f[k, pl.ds(pl.multiple_of(step * 8, 8), 8)]
+            for j in range(8):
+                lanes = pl.ds(pl.multiple_of(step * 8 * blk + j * blk, blk), blk)
+                acc = acc + integrals[:, lanes].astype(F32) * rows_of[j : j + 1]
+            return acc
+
+        acc = lax.fori_loop(0, blk // 8, body, jnp.zeros((count_aux, blk), F32))
+        wide = jnp.concatenate([acc, jnp.zeros((blk - count_aux, blk), F32)], axis=0)
+        part[pl.ds(k, 1)] = jnp.sum(wide.T, axis=0, keepdims=True)
+
+    top, low = pl.ds(0, blk // 2), pl.ds(blk // 2, blk // 2)
+    part[...] = jnp.zeros_like(part)
+    piece_of(0)
+    whole_x = spread(piece.at[0], got_x.at[0], xs, fx_send.at[0], fx_recv.at[0], over_x)
+    piece_x[0] = added(piece.at[0], got_x.at[0], whole_x)
+    whole_y = spread(piece_x.at[0], got_y.at[0], ys, fy_send.at[0], fy_recv.at[0], over_y)
+    piece_of(1)
+    top_x = spread(piece.at[1, top], got_x.at[1, :, top], xs, fx_send.at[1], fx_recv.at[1], over_x)
+    low_y = spread(piece.at[1, low], got_y.at[1, :, low], ys, fy_send.at[2], fy_recv.at[2], over_y)
+    piece_y[0] = added(piece_x.at[0], got_y.at[0], whole_y)
+    whole_c = spread(piece_y.at[0], got_c.at[0], 2, fc_send.at[0], fc_recv.at[0], other_core)
+    piece_x[1, top] = added(piece.at[1, top], got_x.at[1, :, top], top_x)
+    top_y = spread(piece_x.at[1, top], got_y.at[1, :, top], ys, fy_send.at[1], fy_recv.at[1], over_y)
+    piece_x[1, low] = added(piece.at[1, low], got_y.at[1, :, low], low_y)
+    low_x = spread(piece_x.at[1, low], got_x.at[1, :, low], xs, fx_send.at[2], fx_recv.at[2], over_x)
+    piece_f[0] = added(piece_y.at[0], got_c.at[0], whole_c).astype(F32)
     load_t.wait()
-    count_aux = integrals.shape[0]
-
-    def contract(step, carry):
-        acc0, acc1 = carry
-        base = pl.multiple_of(step * 8, 8)
-        rows0 = piece_f[0, pl.ds(base, 8)]
-        rows1 = piece_f[1, pl.ds(base, 8)]
-        for j in range(8):
-            lanes = pl.ds(pl.multiple_of(step * 8 * blk + j * blk, blk), blk)
-            slab = integrals[:, lanes].astype(F32)
-            acc0 = acc0 + slab * rows0[j : j + 1]
-            acc1 = acc1 + slab * rows1[j : j + 1]
-        return acc0, acc1
-
-    zero = jnp.zeros((count_aux, blk), F32)
-    acc = lax.fori_loop(0, blk // 8, contract, (zero, zero))
-    part[...] = jnp.zeros_like(part)
-    for k in range(2):
-        wide = jnp.concatenate([acc[k], jnp.zeros((blk - count_aux, blk), F32)], axis=0)
-        part[pl.ds(k, 1)] = jnp.sum(wide.T, axis=0, keepdims=True)
+    contract(0)
+    piece_y[1, top] = added(piece_x.at[1, top], got_y.at[1, :, top], top_y)
+    top_c = spread(piece_y.at[1, top], got_c.at[1, :, top], 2, fc_send.at[1], fc_recv.at[1], other_core)
+    piece_y[1, low] = added(piece_x.at[1, low], got_x.at[1, :, low], low_x)
+    low_c = spread(piece_y.at[1, low], got_c.at[1, :, low], 2, fc_send.at[2], fc_recv.at[2], other_core)
+    piece_f[1, top] = added(piece_y.at[1, top], got_c.at[1, :, top], top_c).astype(F32)
+    piece_f[1, low] = added(piece_y.at[1, low], got_c.at[1, :, low], low_c).astype(F32)
+    contract(1)
 
     parts_z[z] = part[...]
     z_copies = [
@@ -388,6 +398,27 @@
     for c in h_copies:
         c.wait_recv()
 
+    load_m.wait()
+    lane = lax.broadcasted_iota(jnp.int32, (8, blk), 1)
+    acc = [jnp.zeros((count_aux, blk), F32) for _ in range(2)]
+    for group_of in range(naux // 4):
+        one, two, three, four = (sums[4 * group_of + j] for j in range(4))
+        two = pltpu.roll(two, 96, 1)
+        three = pltpu.roll(three, 64, 1)
+        four = pltpu.roll(four, 32, 1)
+        filled = (
+            jnp.where(lane < 96, one, two),
+            jnp.where(lane < 64, two, three),
+            jnp.where(lane < 32, three, four),
+        )
+        for j, values in enumerate(filled):
+            block = metric[:, pl.ds((3 * group_of + j) * blk, blk)]
+            for k in range(2):
+                acc[k] = acc[k] + block * values[k : k + 1]
+    for k in range(2):
+        wide = jnp.concatenate([acc[k], jnp.zeros((blk - count_aux, blk), F32)], axis=0)
+        coefficients[0, pl.ds(k, 1)] = jnp.sum(wide.T, axis=0, keepdims=True)[:, :count_aux]
+
     for c in pending + z_copies + g_copies + h_copies:
         c.wait_send()
     for r in range(rows):
@@ -432,15 +463,17 @@
         in_hbm = pl.BlockSpec(memory_space=pltpu.HBM)
         smem = pl.BlockSpec(memory_space=pltpu.SMEM)
         in_vmem = pl.BlockSpec(memory_space=pltpu.VMEM)
-        response, sums = pl.pallas_call(
+        return pl.pallas_call(
             functools.partial(ring_kernel, (ys, xs, zs, rows, slots)),
             out_shape=(
                 jax.ShapeDtypeStruct(field_terms.shape, BF16),
-                jax.ShapeDtypeStruct((naux, 8, blk), F32),
+                jax.ShapeDtypeStruct((1, 2, count_aux), F32),
             ),
-            in_specs=[smem, smem, in_hbm, in_hbm, in_hbm],
+            in_specs=[smem, smem, in_hbm, in_hbm, in_hbm, in_hbm],
             out_specs=(in_vmem, in_vmem),
             scratch_shapes=[
+                vmem((naux, 8, blk), F32),
+                vmem((count_aux, naux * count_aux), F32),
                 vmem((3, rows, *block), BF16),
                 vmem((rows, 8, blk), jnp.int32),
                 vmem((slots, 8, blk), jnp.int32),
@@ -459,14 +492,14 @@
                 vmem((2, *block), F32),
                 vmem((8, blk), F32),
                 vmem((zs, 8, blk), F32),
-                dma((4,)),
+                dma((5,)),
                 dma((3, rows)), dma((3, slots)),
                 dma((rows,)), dma((slots,)),
                 dma((2, 3, slots)), dma((2, 3, slots)),
                 dma((2, slots)), dma((2, rows)),
-                dma((2, max(xs - 1, 1))), dma((2, max(xs - 1, 1))),
-                dma((2, max(ys - 1, 1))), dma((2, max(ys - 1, 1))),
-                dma((2, 1)), dma((2, 1)),
+                dma((3, max(xs - 1, 1))), dma((3, max(xs - 1, 1))),
+                dma((3, max(ys - 1, 1))), dma((3, max(ys - 1, 1))),
+                dma((3, 1)), dma((3, 1)),
                 dma((zs,)), dma((zs,)),
                 dma((2 * xs,)), dma((2 * xs,)),
                 dma((max(ys - 1, 1),)), dma((max(ys - 1, 1),)),
@@ -476,11 +509,8 @@
             ),
         )(
             band_pattern, fit_blocks, density_in, field_terms,
-            tensor.reshape(count_aux, blk * blk),
+            tensor.reshape(count_aux, blk * blk), metric_inv,
         )
-        full = sums[:, :2, :count_aux].transpose(1, 0, 2).reshape(1, 2, naux * count_aux)
-        coefficients = jnp.einsum("fpq,fkq->fkp", metric_inv, full, precision=lax.Precision.HIGHEST)
-        return response, coefficients
 
     in_specs = (
         P("aux", None),

time: 170 us -> 130 us (0.76)
  Pallas kernels: 165 us -> 126 us
    pallas_call x1, Pallas kernels: 165 us -> 126 us  [on_device(): pl.pallas_call(functools.partial(ring_kernel, (ys, xs, zs, rows, slots)),...]
    unnamed x5 -> x2, local copies, waits for them, and re-layouts: 0.81 us -> 3.08 us
where the time goes in v3:
time: 130 us
  Pallas kernels  126 us (97%)
  local copies, waits for them, and re-layouts  3.08 us (2%)
    pallas_call x1, Pallas kernels, on_device(): pl.pallas_call(functools.partial(ring_kernel, (ys, xs, zs, rows, slots)),...  126 us
    unnamed x2, local copies, waits for them, and re-layouts  3.08 us

profile of v3, /device:TPU:1, one launch (start us, length us, event | category | flops | bytes accessed | tf_op | source)
XLA Modules:
  0.0 130.2 jit_solution(6788928136565471676)
XLA Ops:
  1.3 125.9 %shard_map.77 = (bf16[2,8,1,128,128]{4,3,2,1,0:T(8,128)(2,1)}, f32[1,2,96]{2,1,0:T(2,128)}) custom-call(s32[8,8]{1,0:T(8,128)} %pattern.1, s32[1]{0:T(128)S(6)} %copy.10.fit_blocks, bf16[8,1,128,128]{3,2,1,0:T(8,128)(2,1)} %density_hbm.1, bf16[2,8,1,128,128]{4,3,2,1,0:T(8,128)(2,1)} %fields_hbm.1, bf16[96,16384]{1,0:T(8,128)(2,1)} %bitcast.1, ...), custom_call_target="tpu_custom_call" | custom-call | tf_op jit(solution)/shard_map/pallas_call | solution.py:466
  127.1 1.9 %copy.11 = bf16[2,8,1,128,128]{4,3,2,1,0:T(8,128)(2,1)} copy(bf16[2,8,1,128,128]{4,3,2,1,0:T(8,128)(2,1)} %get-tuple-element.4) | data formatting | bytes 1048576
  129.0 1.2 copy.12

commit v4 on v3

--- a/solution.py
+++ b/solution.py
@@ -17,11 +17,11 @@
     pattern, fit_blocks, density_hbm, fields_hbm, tensor_hbm, metric_hbm,
     out, coefficients, sums, metric,
     staged, keep_src, keep, win1, win2, lhs1, lhs2, result,
-    integrals, piece, piece_x, piece_y, got_x, got_y, got_c, piece_f, part, parts_z,
+    integrals, piece, piece_x, got_x, got_y, piece_f, part, parts_z,
     load_sem, in_send, in_recv, keep_send, keep_recv,
     win_send, win_recv,
     out_send, out_recv,
-    fx_send, fx_recv, fy_send, fy_recv, fc_send, fc_recv,
+    fx_send, fx_recv, fy_send, fy_recv,
     z_send, z_recv, g_send, g_recv, h_send, h_recv,
 ):
     ys, xs, zs, rows, slots = sizes
@@ -78,32 +78,35 @@
     def greet(a, b):
         pl.semaphore_signal(barrier, inc=1, device_id={"aux": a, "orb": b}, device_id_type=MESH)
 
-    self_holds = src_aux == aux
-    for r in range(rows):
-        to_aux, to_z = dest_of(r)
-
-        @pl.when(jnp.logical_not((to_aux == aux) & (to_z == z)))
+    for step in range(1, 2 * zs):
+        e = (2 * z + core + step) % (2 * zs)
+        greet(2 * col + e % 2, e // 2)
+    greeted += 2 * zs - 1
+    for offset in (-2, -1, 1, 2):
+        to_aux, to_z = holder(row + offset)
+
+        @pl.when(to_aux // 2 != col)
         def _():
             greet(to_aux, to_z)
 
-    for s in range(zs):
-        @pl.when(jnp.logical_not((src_aux == aux) & (z == s)))
-        def _():
-            greet(src_aux, s)
-
-    greeted += rows + zs
-    for offset in (-2, -1, 1, 2):
-        greet(*holder(row + offset))
-    greeted += 4
-    for step in range(1, zs):
-        greet(aux, (z + step) % zs)
-    greeted += zs - 1
+    place = row % (2 * zs)
+    near_end = (place < 2) | (place >= 2 * zs - 2)
+    at_end = (place < 1) | (place >= 2 * zs - 1)
     for step in range(1, 2 * xs):
-        greet(2 * xs * y + (2 * x + core + step) % (2 * xs), z)
-    greeted += 2 * xs - 1
-    for step in range(1, ys):
-        greet(2 * (((y + step) % ys) * xs + x) + core, z)
-        greeted += 1
+        e = (2 * x + core + step) % (2 * xs)
+
+        @pl.when(e // 2 != x)
+        def _():
+            greet(2 * xs * y + e, z)
+
+    for step in range(1, 2 * ys):
+        e = (2 * y + core + step) % (2 * ys)
+
+        @pl.when(e // 2 != y)
+        def _():
+            greet(2 * (e // 2 * xs + x) + e % 2, z)
+
+    greeted += 2 * (xs - 1) + 2 * (ys - 1)
 
     first_row = aux * rows
     column = first_row + z - half
@@ -120,7 +123,7 @@
         factor = jnp.full((blk, blk), mask_of(r).astype(F32), F32).astype(BF16)
         staged[0, r] = staged[0, r] * factor
 
-    pl.semaphore_wait(barrier, greeted - jnp.where(self_holds, 2, 0))
+    pl.semaphore_wait(barrier, greeted + jnp.where(near_end, 1, 0) + jnp.where(at_end, 1, 0))
 
     def send_in(mat, r):
         to_aux, to_z = dest_of(r)
@@ -265,25 +268,27 @@
         lax.fori_loop(0, slots, body, 0)
 
     done = 4
-    first_wave = (0, 1, 2, 3, 4, 5)
-    for wave in range(first_wave[-1] + done):
-        for item in range(6):
-            step = wave - first_wave[item] + 1
-            if step < 1 or step > done:
-                continue
-            phase, mat = item // 3, item % 3
-            if step == 1 and phase == 0:
-                arrived(mat)
-            if step == 1 and phase == 1:
-                if mat == 0:
-                    for u in range(slots):
-                        landed(keep.at[u], keep_recv.at[u])
-                    square()
-                else:
-                    first(mat - 1)
-            advance(win1 if phase == 0 else win2, phase, mat, step)
-            if step == done and phase == 1 and mat > 0:
-                second(mat - 1)
+    order = (
+        "D1", "P1", "D2", "S1", "P2", "D3", "D4", "Q1",
+        "S2", "P3", "P4", "F1", "Q2", "S3", "S4", "G1",
+        "F2", "Q3", "G2", "F3", "Q4", "F4", "G3", "G4",
+    )
+    item_of = {"D": 0, "P": 1, "S": 2, "Q": 3, "F": 4, "G": 5}
+    for word in order:
+        item, step = item_of[word[0]], int(word[1])
+        phase, mat = item // 3, item % 3
+        if step == 1 and phase == 0:
+            arrived(mat)
+        if step == 1 and phase == 1:
+            if mat == 0:
+                for u in range(slots):
+                    landed(keep.at[u], keep_recv.at[u])
+                square()
+            else:
+                first(mat - 1)
+        advance(win1 if phase == 0 else win2, phase, mat, step)
+        if step == done and phase == 1 and mat > 0:
+            second(mat - 1)
 
     fitted = fit_blocks[0]
 
@@ -321,9 +326,6 @@
             value = value + out[k, r, 0] * jnp.full((blk, blk), chosen, F32).astype(BF16)
         piece[k] = value
 
-    def other_core(d):
-        return aux + 1 - 2 * core
-
     count_aux = integrals.shape[0]
 
     def contract(k):
@@ -338,30 +340,30 @@
         wide = jnp.concatenate([acc, jnp.zeros((blk - count_aux, blk), F32)], axis=0)
         part[pl.ds(k, 1)] = jnp.sum(wide.T, axis=0, keepdims=True)
 
+    def x_cores(d):
+        return 2 * xs * y + (2 * x + core + d) % (2 * xs)
+
+    def y_cores(d):
+        e = (2 * y + core + d) % (2 * ys)
+        return 2 * (e // 2 * xs + x) + e % 2
+
     top, low = pl.ds(0, blk // 2), pl.ds(blk // 2, blk // 2)
-    part[...] = jnp.zeros_like(part)
     piece_of(0)
-    whole_x = spread(piece.at[0], got_x.at[0], xs, fx_send.at[0], fx_recv.at[0], over_x)
-    piece_x[0] = added(piece.at[0], got_x.at[0], whole_x)
-    whole_y = spread(piece_x.at[0], got_y.at[0], ys, fy_send.at[0], fy_recv.at[0], over_y)
+    whole_1 = spread(piece.at[0], got_x.at[0], 2 * xs, fx_send.at[0], fx_recv.at[0], x_cores)
+    piece_x[0] = added(piece.at[0], got_x.at[0], whole_1)
+    whole_2 = spread(piece_x.at[0], got_y.at[0], ys, fy_send.at[0], fy_recv.at[0], over_y)
     piece_of(1)
-    top_x = spread(piece.at[1, top], got_x.at[1, :, top], xs, fx_send.at[1], fx_recv.at[1], over_x)
-    low_y = spread(piece.at[1, low], got_y.at[1, :, low], ys, fy_send.at[2], fy_recv.at[2], over_y)
-    piece_y[0] = added(piece_x.at[0], got_y.at[0], whole_y)
-    whole_c = spread(piece_y.at[0], got_c.at[0], 2, fc_send.at[0], fc_recv.at[0], other_core)
-    piece_x[1, top] = added(piece.at[1, top], got_x.at[1, :, top], top_x)
-    top_y = spread(piece_x.at[1, top], got_y.at[1, :, top], ys, fy_send.at[1], fy_recv.at[1], over_y)
-    piece_x[1, low] = added(piece.at[1, low], got_y.at[1, :, low], low_y)
-    low_x = spread(piece_x.at[1, low], got_x.at[1, :, low], xs, fx_send.at[2], fx_recv.at[2], over_x)
-    piece_f[0] = added(piece_y.at[0], got_c.at[0], whole_c).astype(F32)
+    top_1 = spread(piece.at[1, top], got_x.at[1, :, top], 2 * xs, fx_send.at[1], fx_recv.at[1], x_cores)
+    low_1 = spread(piece.at[1, low], got_x.at[1, :, low], 2 * ys, fx_send.at[2], fx_recv.at[2], y_cores)
+    piece_f[0] = added(piece_x.at[0], got_y.at[0], whole_2).astype(F32)
+    piece_x[1, top] = added(piece.at[1, top], got_x.at[1, :, top], top_1)
+    top_2 = spread(piece_x.at[1, top], got_y.at[1, :, top], ys, fy_send.at[1], fy_recv.at[1], over_y)
+    piece_x[1, low] = added(piece.at[1, low], got_x.at[1, :, low], low_1)
+    low_2 = spread(piece_x.at[1, low], got_y.at[1, :, low], xs, fy_send.at[2], fy_recv.at[2], over_x)
     load_t.wait()
     contract(0)
-    piece_y[1, top] = added(piece_x.at[1, top], got_y.at[1, :, top], top_y)
-    top_c = spread(piece_y.at[1, top], got_c.at[1, :, top], 2, fc_send.at[1], fc_recv.at[1], other_core)
-    piece_y[1, low] = added(piece_x.at[1, low], got_x.at[1, :, low], low_x)
-    low_c = spread(piece_y.at[1, low], got_c.at[1, :, low], 2, fc_send.at[2], fc_recv.at[2], other_core)
-    piece_f[1, top] = added(piece_y.at[1, top], got_c.at[1, :, top], top_c).astype(F32)
-    piece_f[1, low] = added(piece_y.at[1, low], got_c.at[1, :, low], low_c).astype(F32)
+    piece_f[1, top] = added(piece_x.at[1, top], got_y.at[1, :, top], top_2).astype(F32)
+    piece_f[1, low] = added(piece_x.at[1, low], got_y.at[1, :, low], low_2).astype(F32)
     contract(1)
 
     parts_z[z] = part[...]
@@ -399,22 +401,23 @@
         c.wait_recv()
 
     load_m.wait()
-    lane = lax.broadcasted_iota(jnp.int32, (8, blk), 1)
+    lane = lax.broadcasted_iota(jnp.int32, (1, blk), 1)
     acc = [jnp.zeros((count_aux, blk), F32) for _ in range(2)]
     for group_of in range(naux // 4):
-        one, two, three, four = (sums[4 * group_of + j] for j in range(4))
-        two = pltpu.roll(two, 96, 1)
-        three = pltpu.roll(three, 64, 1)
-        four = pltpu.roll(four, 32, 1)
-        filled = (
-            jnp.where(lane < 96, one, two),
-            jnp.where(lane < 64, two, three),
-            jnp.where(lane < 32, three, four),
-        )
-        for j, values in enumerate(filled):
-            block = metric[:, pl.ds((3 * group_of + j) * blk, blk)]
-            for k in range(2):
-                acc[k] = acc[k] + block * values[k : k + 1]
+        pieces = jnp.concatenate([sums[4 * group_of + j] for j in range(4)], axis=0)
+        by96, by64, by32 = (pltpu.roll(pieces, shift, 1) for shift in (96, 64, 32))
+        for k in range(2):
+            one = pieces[k : k + 1]
+            two = by96[2 + k : 3 + k]
+            three = by64[4 + k : 5 + k]
+            four = by32[6 + k : 7 + k]
+            filled = (
+                jnp.where(lane < 96, one, two),
+                jnp.where(lane < 64, two, three),
+                jnp.where(lane < 32, three, four),
+            )
+            for j, values in enumerate(filled):
+                acc[k] = acc[k] + metric[:, pl.ds((3 * group_of + j) * blk, blk)] * values
     for k in range(2):
         wide = jnp.concatenate([acc[k], jnp.zeros((blk - count_aux, blk), F32)], axis=0)
         coefficients[0, pl.ds(k, 1)] = jnp.sum(wide.T, axis=0, keepdims=True)[:, :count_aux]
@@ -472,7 +475,7 @@
             in_specs=[smem, smem, in_hbm, in_hbm, in_hbm, in_hbm],
             out_specs=(in_vmem, in_vmem),
             scratch_shapes=[
-                vmem((naux, 8, blk), F32),
+                vmem((naux, 2, blk), F32),
                 vmem((count_aux, naux * count_aux), F32),
                 vmem((3, rows, *block), BF16),
                 vmem((rows, 8, blk), jnp.int32),
@@ -485,21 +488,18 @@
                 vmem((count_aux, blk * blk), BF16),
                 vmem((2, *block), BF16),
                 vmem((2, *block), BF16),
-                vmem((2, *block), BF16),
-                vmem((2, max(xs - 1, 1), *block), BF16),
-                vmem((2, max(ys - 1, 1), *block), BF16),
-                vmem((2, 1, *block), BF16),
+                vmem((2, 2 * max(xs, ys) - 1, *block), BF16),
+                vmem((2, max(xs, ys) - 1, *block), BF16),
                 vmem((2, *block), F32),
-                vmem((8, blk), F32),
-                vmem((zs, 8, blk), F32),
+                vmem((2, blk), F32),
+                vmem((zs, 2, blk), F32),
                 dma((5,)),
                 dma((3, rows)), dma((3, slots)),
                 dma((rows,)), dma((slots,)),
                 dma((2, 3, slots)), dma((2, 3, slots)),
                 dma((2, slots)), dma((2, rows)),
-                dma((3, max(xs - 1, 1))), dma((3, max(xs - 1, 1))),
-                dma((3, max(ys - 1, 1))), dma((3, max(ys - 1, 1))),
-                dma((3, 1)), dma((3, 1)),
+                dma((3, 2 * max(xs, ys) - 1)), dma((3, 2 * max(xs, ys) - 1)),
+                dma((3, max(xs, ys) - 1)), dma((3, max(xs, ys) - 1)),
                 dma((zs,)), dma((zs,)),
                 dma((2 * xs,)), dma((2 * xs,)),
                 dma((max(ys - 1, 1),)), dma((max(ys - 1, 1),)),

time: 130 us -> 119 us (0.915)
  Pallas kernels: 126 us -> 115 us
    pallas_call x1, Pallas kernels: 126 us -> 115 us  [on_device(): pl.pallas_call(functools.partial(ring_kernel, (ys, xs, zs, rows, slots)),...]
where the time goes in v4:
time: 119 us
  Pallas kernels  115 us (97%)
  local copies, waits for them, and re-layouts  3.08 us (3%)
  between operations  1.29 us (1%)
    pallas_call x1, Pallas kernels, on_device(): pl.pallas_call(functools.partial(ring_kernel, (ys, xs, zs, rows, slots)),...  115 us
    unnamed x2, local copies, waits for them, and re-layouts  3.08 us

profile of v4, /device:TPU:1, one launch (start us, length us, event | category | flops | bytes accessed | tf_op | source)
XLA Modules:
  0.0 119.1 jit_solution(15604028534102680965)
XLA Ops:
  1.3 114.7 %shard_map.77 = (bf16[2,8,1,128,128]{4,3,2,1,0:T(8,128)(2,1)}, f32[1,2,96]{2,1,0:T(2,128)}) custom-call(s32[8,8]{1,0:T(8,128)} %pattern.1, s32[1]{0:T(128)S(6)} %copy.10.fit_blocks, bf16[8,1,128,128]{3,2,1,0:T(8,128)(2,1)} %density_hbm.1, bf16[2,8,1,128,128]{4,3,2,1,0:T(8,128)(2,1)} %fields_hbm.1, bf16[96,16384]{1,0:T(8,128)(2,1)} %bitcast.1, ...), custom_call_target="tpu_custom_call" | custom-call | tf_op jit(solution)/shard_map/pallas_call | solution.py:469
  116.0 1.9 %copy.11 = bf16[2,8,1,128,128]{4,3,2,1,0:T(8,128)(2,1)} copy(bf16[2,8,1,128,128]{4,3,2,1,0:T(8,128)(2,1)} %get-tuple-element.4) | data formatting | bytes 1048576
  117.9 1.2 %copy.12 = f32[1,2,96]{2,1,0:T(2,128)} copy(f32[1,2,96]{2,1,0:T(2,128)} %get-tuple-element.5) | data formatting | bytes 1536

commit v5 on v4

--- a/solution.py
+++ b/solution.py
@@ -22,7 +22,7 @@
     win_send, win_recv,
     out_send, out_recv,
     fx_send, fx_recv, fy_send, fy_recv,
-    z_send, z_recv, g_send, g_recv, h_send, h_recv,
+    z_send, z_recv, g_send, g_recv,
 ):
     ys, xs, zs, rows, slots = sizes
     half = slots // 2
@@ -106,7 +106,14 @@
         def _():
             greet(2 * (e // 2 * xs + x) + e % 2, z)
 
-    greeted += 2 * (xs - 1) + 2 * (ys - 1)
+    for step in range(1, xs * ys):
+        c = (col + step) % (xs * ys)
+
+        @pl.when((c % xs != x) & (c // xs != y))
+        def _():
+            greet(2 * c + core, z)
+
+    greeted += 2 * (xs - 1) + 2 * (ys - 1) + (xs - 1) * (ys - 1)
 
     first_row = aux * rows
     column = first_row + z - half
@@ -366,38 +373,29 @@
     piece_f[1, low] = added(piece_x.at[1, low], got_y.at[1, :, low], low_2).astype(F32)
     contract(1)
 
-    parts_z[z] = part[...]
-    z_copies = [
-        remote(part, parts_z.at[z], z_send.at[d - 1], z_recv.at[d - 1], aux, (z + d) % zs)
-        for d in range(1, zs)
-    ]
+    e = 2 * z + core
+    parts_z[e] = part[...]
+    z_copies = []
+    for d in range(1, 2 * zs):
+        f = (e + d) % (2 * zs)
+        z_copies.append(remote(part, parts_z.at[e], z_send.at[d - 1], z_recv.at[d - 1], 2 * col + f % 2, f // 2))
     for c in z_copies:
         c.start()
     for c in z_copies:
         c.wait_recv()
-    total = parts_z[0]
-    for d in range(1, zs):
-        total = total + parts_z[d]
-    sums[aux] = total
-
-    group = 2 * xs
-    e = 2 * x + core
+    for c in range(2):
+        total = parts_z[c]
+        for d in range(1, zs):
+            total = total + parts_z[2 * d + c]
+        sums[2 * col + c] = total
+    mine = sums.at[pl.ds(2 * col, 2)]
     g_copies = [
-        remote(sums.at[aux], sums.at[aux], g_send.at[d - 1], g_recv.at[d - 1], group * y + (e + d) % group, z)
-        for d in range(1, group)
+        remote(mine, mine, g_send.at[d - 1], g_recv.at[d - 1], 2 * ((col + d) % (xs * ys)) + core, z)
+        for d in range(1, xs * ys)
     ]
     for c in g_copies:
         c.start()
     for c in g_copies:
-        c.wait_recv()
-    mine = sums.at[pl.ds(group * y, group)]
-    h_copies = [
-        remote(mine, mine, h_send.at[d - 1], h_recv.at[d - 1], 2 * (((y + d) % ys) * xs + x) + core, z)
-        for d in range(1, ys)
-    ]
-    for c in h_copies:
-        c.start()
-    for c in h_copies:
         c.wait_recv()
 
     load_m.wait()
@@ -422,7 +420,7 @@
         wide = jnp.concatenate([acc[k], jnp.zeros((blk - count_aux, blk), F32)], axis=0)
         coefficients[0, pl.ds(k, 1)] = jnp.sum(wide.T, axis=0, keepdims=True)[:, :count_aux]
 
-    for c in pending + z_copies + g_copies + h_copies:
+    for c in pending + z_copies + g_copies:
         c.wait_send()
     for r in range(rows):
         to_aux, to_z = dest_of(r)
@@ -492,7 +490,7 @@
                 vmem((2, max(xs, ys) - 1, *block), BF16),
                 vmem((2, *block), F32),
                 vmem((2, blk), F32),
-                vmem((zs, 2, blk), F32),
+                vmem((2 * zs, 2, blk), F32),
                 dma((5,)),
                 dma((3, rows)), dma((3, slots)),
                 dma((rows,)), dma((slots,)),
@@ -500,12 +498,11 @@
                 dma((2, slots)), dma((2, rows)),
                 dma((3, 2 * max(xs, ys) - 1)), dma((3, 2 * max(xs, ys) - 1)),
                 dma((3, max(xs, ys) - 1)), dma((3, max(xs, ys) - 1)),
-                dma((zs,)), dma((zs,)),
-                dma((2 * xs,)), dma((2 * xs,)),
-                dma((max(ys - 1, 1),)), dma((max(ys - 1, 1),)),
+                dma((2 * zs,)), dma((2 * zs,)),
+                dma((xs * ys,)), dma((xs * ys,)),
             ],
             compiler_params=pltpu.CompilerParams(
-                collective_id=0, has_side_effects=True, vmem_limit_bytes=62 << 20
+                collective_id=0, has_side_effects=True, vmem_limit_bytes=53 << 20
             ),
         )(
             band_pattern, fit_blocks, density_in, field_terms,

time: 119 us -> 116 us (0.975)
  Pallas kernels: 115 us -> 112 us
    pallas_call x1, Pallas kernels: 115 us -> 112 us  [on_device(): pl.pallas_call(functools.partial(ring_kernel, (ys, xs, zs, rows, slots)),...]
    unnamed x2 -> x6, local copies, waits for them, and re-layouts: 3.08 us -> 2.99 us
where the time goes in v5:
time: 116 us
  Pallas kernels  112 us (97%)
  local copies, waits for them, and re-layouts  2.99 us (3%)
  between operations  1.29 us (1%)
    pallas_call x1, Pallas kernels, on_device(): pl.pallas_call(functools.partial(ring_kernel, (ys, xs, zs, rows, slots)),...  112 us
    unnamed x6, local copies, waits for them, and re-layouts  2.99 us

profile of v5, /device:TPU:1, one launch (start us, length us, event | category | flops | bytes accessed | tf_op | source)
XLA Modules:
  0.0 116.3 jit_solution(8675416724227980559)
XLA Ops:
  1.3 0.0 copy-start
  1.3 0.9 copy-done
  2.2 0.0 copy-start.1
  2.2 0.7 copy-done.1
  2.9 112.1 %shard_map.77 = (bf16[2,8,1,128,128]{4,3,2,1,0:T(8,128)(2,1)S(1)}, f32[1,2,96]{2,1,0:T(2,128)S(1)}) custom-call(s32[8,8]{1,0:T(8,128)S(1)} %copy-done.1, s32[1]{0:T(128)S(6)} %copy.10.fit_blocks, bf16[8,1,128,128]{3,2,1,0:T(8,128)(2,1)S(1)} %copy-done, bf16[2,8,1,128,128]{4,3,2,1,0:T(8,128)(2,1)} %fields_hbm.1, bf16[96,16384]{1,0:T(8,128)(2,1)} %bitcast.1, ...), custom_call_target="tpu_custom_call" | custom-call | tf_op jit(solution)/shard_map/pallas_call | solution.py:467
  115.0 0.8 copy.11
  115.8 0.6 copy.12
Async XLA Ops:
  1.3 1.0 copy-start
  2.2 0.7 copy-start.1

commit v6 on v5

--- a/solution.py
+++ b/solution.py
@@ -169,13 +169,6 @@
         for r in range(rows):
             send_in(1 + k, r)
 
-    for t in range(slots):
-        empty = range(t + half, slots) if t < half else range(0, t - half)
-        for s in empty:
-            for mat in range(3):
-                win1[mat, s, pl.ds(t * blk, blk)] = jnp.zeros((blk, blk), BF16)
-                win2[mat, s, pl.ds(t * blk, blk)] = jnp.zeros((blk, blk), BF16)
-
     def slots_of(t):
         return max(0, t - half), min(slots, t + half)
 
@@ -230,24 +223,30 @@
         mask = jnp.broadcast_to(keep[s, pl.ds(0, 1), :], (blk, blk))
         return jnp.where(mask > 0, value, 0.0)
 
+    def rows_of(s):
+        lo, hi = max(0, s - half + 1), min(slots, s + half + 1)
+        return pl.ds(lo * blk, (hi - lo) * blk)
+
     def square():
         def body(s, carry):
-            value = jnp.dot(lhs1[0], win1[0, s], preferred_element_type=F32)
+            value = jnp.dot(lhs1[0, :, rows_of(s)], win1[0, s, rows_of(s)], preferred_element_type=F32)
             win2[0, s, pl.ds(own_lo, blk)] = kept(s, value).astype(BF16)
             return carry
 
-        lax.fori_loop(0, slots, body, 0)
+        for s in range(slots):
+            body(s, 0)
         for s in range(slots):
             lhs2[0, :, pl.ds(s * blk, blk)] = win2[0, s, pl.ds(own_lo, blk)]
 
     def first(k):
         def body(s, carry):
-            value = jnp.dot(lhs1[0], win1[1 + k, s], preferred_element_type=F32)
-            value = value + jnp.dot(lhs1[1 + k], win1[0, s], preferred_element_type=F32)
+            value = jnp.dot(lhs1[0, :, rows_of(s)], win1[1 + k, s, rows_of(s)], preferred_element_type=F32)
+            value = value + jnp.dot(lhs1[1 + k, :, rows_of(s)], win1[0, s, rows_of(s)], preferred_element_type=F32)
             win2[1 + k, s, pl.ds(own_lo, blk)] = kept(s, value).astype(BF16)
             return carry
 
-        lax.fori_loop(0, slots, body, 0)
+        for s in range(slots):
+            body(s, 0)
         for s in range(slots):
             lhs2[1 + k, :, pl.ds(s * blk, blk)] = win2[1 + k, s, pl.ds(own_lo, blk)]
 
@@ -265,19 +264,20 @@
 
     def second(k):
         def body(s, carry):
-            value = jnp.dot(lhs2[0], win2[1 + k, s], preferred_element_type=F32)
-            value = value + jnp.dot(lhs2[1 + k], win2[0, s], preferred_element_type=F32)
+            value = jnp.dot(lhs2[0, :, rows_of(s)], win2[1 + k, s, rows_of(s)], preferred_element_type=F32)
+            value = value + jnp.dot(lhs2[1 + k, :, rows_of(s)], win2[0, s, rows_of(s)], preferred_element_type=F32)
             value = 2.0 * win2[1 + k, s, pl.ds(own_lo, blk)].astype(F32) - value
             result[k, s] = kept(s, value).astype(BF16)
             send_out(k, s)
             return carry
 
-        lax.fori_loop(0, slots, body, 0)
+        for s in range(slots):
+            body(s, 0)
 
     done = 4
     order = (
         "D1", "P1", "D2", "S1", "P2", "D3", "D4", "Q1",
-        "S2", "P3", "P4", "F1", "Q2", "S3", "S4", "G1",
+        "P3", "S2", "P4", "F1", "Q2", "S3", "S4", "G1",
         "F2", "Q3", "G2", "F3", "Q4", "F4", "G3", "G4",
     )
     item_of = {"D": 0, "P": 1, "S": 2, "Q": 3, "F": 4, "G": 5}

time: 116 us -> 121 us (1.043)
  Pallas kernels: 112 us -> 116 us
    pallas_call x1, Pallas kernels: 112 us -> 116 us  [on_device(): pl.pallas_call(functools.partial(ring_kernel, (ys, xs, zs, rows, slots)),...]
where the time goes in v6:
time: 121 us
  Pallas kernels  116 us (96%)
  local copies, waits for them, and re-layouts  2.99 us (2%)
  between operations  1.29 us (1%)
    pallas_call x1, Pallas kernels, on_device(): pl.pallas_call(functools.partial(ring_kernel, (ys, xs, zs, rows, slots)),...  116 us
    unnamed x6, local copies, waits for them, and re-layouts  2.99 us

profile of v6, /device:TPU:1, one launch (start us, length us, event | category | flops | bytes accessed | tf_op | source)
XLA Modules:
  0.0 120.6 jit_solution(7704471359575909313)
XLA Ops:
  1.3 0.0 copy-start
  1.3 0.9 copy-done
  2.2 0.0 copy-start.1
  2.2 0.7 copy-done.1
  2.9 116.3 %shard_map.77 = (bf16[2,8,1,128,128]{4,3,2,1,0:T(8,128)(2,1)S(1)}, f32[1,2,96]{2,1,0:T(2,128)S(1)}) custom-call(s32[8,8]{1,0:T(8,128)S(1)} %copy-done.1, s32[1]{0:T(128)S(6)} %copy.10.fit_blocks, bf16[8,1,128,128]{3,2,1,0:T(8,128)(2,1)S(1)} %copy-done, bf16[2,8,1,128,128]{4,3,2,1,0:T(8,128)(2,1)} %fields_hbm.1, bf16[96,16384]{1,0:T(8,128)(2,1)} %bitcast.1, ...), custom_call_target="tpu_custom_call" | custom-call | tf_op jit(solution)/shard_map/pallas_call | solution.py:467
  119.2 0.8 copy.11
  120.0 0.6 copy.12
Async XLA Ops:
  1.3 1.0 copy-start
  2.2 0.7 copy-start.1
